TPU v7x, 256 devices: a whole 4x4x8 slice. The times are simulated.
256 devices in a mesh: lat: 8 (over z), lon: 32 (over y, x, core).
Axes of the slice: x: 4, y: 4, z: 8, core: 2. Of those that a mesh axis runs over, the one named last changes fastest.
Arguments:
- u_wind: float32 [1440, 32, 128], P('lon', 'lat'), may hold values from -6 to 6
- v_wind: float32 [1440, 32, 128], P('lon', 'lat'), may hold values from -6 to 6
- height: float32 [1440, 32, 128], P('lon', 'lat'), may hold values from -6 to 6
- wave_speed: float32 [128], replicated, may hold values from 0.1 to 0.4
- cutoff: int32 [32], replicated, may hold values from 1 to 720, as said below
Outputs:
- u_next: float32 [1440, 32, 128], P('lon', 'lat')
- v_next: float32 [1440, 32, 128], P('lon', 'lat')
- h_next: float32 [1440, 32, 128], P('lon', 'lat')
Inputs may be any that keep to these rules, and one draw needn't show every extreme that they name: `cutoff`: rows 8 to 23, within 45 degrees of the equator, hold 720, which keeps every wavenumber; the other rows hold smaller values, 1 on the two outermost rows.
All inputs are finite; a program needn't handle non-finite values.
Results may differ from a plain program's by a relative error of at most 0.00005.
Values sent between devices are 32-bit elements; how exact they have to be, the bound alone decides.
No kernel may reach another device: no remote copies, remote signals or barrier semaphores. Data moves between devices by JAX's collectives and lax.ppermute only.
A program may use at most 64 MiB of HBM per device.

v0:
```python
import math

import jax
import jax.numpy as jnp
import ml_dtypes
import numpy as np
from jax import lax
from jax.experimental import pallas as pl
from jax.experimental.pallas import tpu as pltpu
from jax.sharding import Mesh
from jax.sharding import PartitionSpec as P

LON = ("lon_0", "lon_1", "lon_2")

NB = 32
NR = 45
PTS = NB * NR
NK = NB // 2 + 1
PAIRS = (NK + 1) // 2
ROWS = 4
HALO = 3
LV = 4
FAR = 1 << 20
PARAMS = pltpu.CompilerParams(vmem_limit_bytes=12 << 20)


def split_three(a):
    high = a.astype(ml_dtypes.bfloat16)
    rest = a - high.astype(np.float64)
    mid = rest.astype(ml_dtypes.bfloat16)
    low = (rest - mid.astype(np.float64)).astype(ml_dtypes.bfloat16)
    return high, mid, low


def host_tables(bands):
    r = np.arange(NR)
    ang = 2.0 * np.pi * np.outer(r, r) / NR
    dft = np.zeros((128, 256))
    twid = np.zeros((NK, 2, 128))
    for side in range(2):
        at = slice(side * 64, side * 64 + NR)
        dft[at, at] = np.cos(ang)
        dft[at, 128 + side * 64 : 128 + side * 64 + NR] = np.sin(ang)
        for k in range(NK):
            twid[k, 0, at] = np.cos(2.0 * np.pi * k * r / PTS)
            twid[k, 1, at] = np.sin(2.0 * np.pi * k * r / PTS)
    high, mid, low = split_three(dft)
    dft = np.concatenate([high, high, mid, mid, low, high], axis=0)
    lane = np.arange(128)
    k1 = 2 * np.arange(PAIRS)[:, None] + lane[None, :] // 64
    wav = k1 + NB * (lane % 64)[None, :]
    ok = (k1 < NK) & (lane % 64 < NR)[None, :]
    slope = np.where(ok, np.sin(2.0 * np.pi * wav / PTS), 0.0)
    least = np.where(ok, np.minimum(wav, PTS - wav), FAR)
    total = bands * ROWS
    per_band = np.zeros((bands, 4, 16, 128), np.float32)
    row = np.arange(-HALO, ROWS + HALO)
    half_pi = np.float32(0.5 * math.pi)
    for z in range(bands):
        g = z * ROWS + row
        ok = (g >= 0) & (g < total)
        lat = half_pi - (g.astype(np.float32) + np.float32(0.5)) * np.float32(math.pi / total)
        cos = np.where(ok, np.cos(lat, dtype=np.float32), np.float32(1.0))
        sin = np.sin(lat, dtype=np.float32)
        rows = (0.25 * sin, PTS / (2.0 * total) / cos, cos, 0.5 / cos)
        for c, value in enumerate(rows):
            per_band[z, c, : len(row), :] = np.where(ok, value, 0.0)[:, None]
    f32 = lambda a: jnp.asarray(np.asarray(a, np.float32))
    return (
        jnp.asarray(dft),
        f32(twid),
        f32(twid / PTS),
        f32(slope[:, None, :]),
        jnp.asarray(least[:, None, :].astype(np.int32)),
        f32(per_band),
    )


def real_fft(xs):
    n = len(xs)
    if n == 1:
        return [(xs[0], None)]
    even, odd = real_fft(xs[0::2]), real_fft(xs[1::2])
    out = [None] * (n // 2 + 1)
    for k in range(n // 4 + 1 if n > 2 else 1):
        er, ei = even[k]
        orr, oi = odd[k]
        if k == 0:
            out[0] = (er + orr, None)
            out[n // 2] = (er - orr, None)
        elif 4 * k == n:
            out[k] = (er, -orr)
        else:
            c, s = math.cos(2 * math.pi * k / n), math.sin(2 * math.pi * k / n)
            if oi is None:
                tr, ti = orr * c, orr * (-s)
            elif 8 * k == n:
                tr, ti = (orr + oi) * c, (oi - orr) * c
            else:
                tr, ti = orr * c + oi * s, oi * c - orr * s
            if ei is None:
                out[k] = (er + tr, ti)
                out[n // 2 - k] = (er - tr, ti)
            else:
                out[k] = (er + tr, ei + ti)
                out[n // 2 - k] = (er - tr, ti - ei)
    return out


def real_ifft(spec):
    n = 2 * (len(spec) - 1)
    if n == 2:
        return [spec[0][0] + spec[1][0], spec[0][0] - spec[1][0]]
    even, odd = [None] * (n // 4 + 1), [None] * (n // 4 + 1)
    for k in range(n // 4 + 1):
        ar, ai = spec[k]
        if k == 0:
            br = spec[n // 2][0]
            even[0] = (ar + br, None)
            odd[0] = (ar - br, None)
        elif 4 * k == n:
            even[k] = (2.0 * ar, None)
            odd[k] = (-2.0 * ai, None)
        else:
            br, bi = spec[n // 2 - k]
            even[k] = (ar + br, ai - bi)
            dr, di = ar - br, ai + bi
            c, s = math.cos(2 * math.pi * k / n), math.sin(2 * math.pi * k / n)
            if 8 * k == n:
                odd[k] = ((dr - di) * c, (dr + di) * c)
            else:
                odd[k] = (dr * c - di * s, dr * s + di * c)
    xe, xo = real_ifft(even), real_ifft(odd)
    out = []
    for a, b in zip(xe, xo):
        out += [a, b]
    return out


def pack_kernel(u_hbm, v_hbm, h_hbm, cut_hbm, speed_hbm, o_ref, cut_ref, speed_ref, raw, tmp, cut, speed, sem):
    copies = [
        pltpu.make_async_copy(src, raw.at[f], sem.at[f])
        for f, src in enumerate((u_hbm, v_hbm, h_hbm))
    ]
    copies.append(pltpu.make_async_copy(cut_hbm, cut, sem.at[3]))
    copies.append(pltpu.make_async_copy(speed_hbm, speed, sem.at[4]))
    for copy in copies:
        copy.start()
    tmp[...] = jnp.zeros_like(tmp)
    for f in range(3):
        copies[f].wait()
        for j in range(ROWS):
            tmp[f, j // 2, j % 2 * 64 : j % 2 * 64 + NR, :] = raw[f, :, j, :]
        for half in range(2):
            turned = tmp[f, half].T
            for l in range(LV):
                o_ref[:, half * LV + l, f * 128 : (f + 1) * 128] = turned[l * NB : (l + 1) * NB, :]
    copies[3].wait()
    copies[4].wait()
    z = lax.axis_index("lat")
    p = (lax.axis_index("lon_0") * 4 + lax.axis_index("lon_1")) * 2 + lax.axis_index("lon_2")
    total = cut.shape[0]
    sub = lax.broadcasted_iota(jnp.int32, (16, 128), 0)
    rows = jnp.full((16, 128), -1, jnp.int32)
    for i in range(ROWS + 2 * HALO):
        g = z * ROWS + i - HALO
        inside = jnp.logical_and(g >= 0, g < total)
        rows = jnp.where(sub == i, jnp.where(inside, cut[jnp.clip(g, 0, total - 1)], -1), rows)
    cut_ref[...] = rows
    sub = lax.broadcasted_iota(jnp.int32, (8, 128), 0)
    value = jnp.zeros((8, 128), jnp.float32)
    for l in range(LV):
        value = jnp.where(sub % LV == l, speed[l * NB + p], value)
    speed_ref[...] = value


def split_store(ref, at, re, im):
    x = jnp.concatenate([re, im], axis=0)
    high = x.astype(jnp.bfloat16)
    rest = x - high.astype(jnp.float32)
    mid = rest.astype(jnp.bfloat16)
    low = (rest - mid.astype(jnp.float32)).astype(jnp.bfloat16)
    for i, part in enumerate((high, mid, high, mid, high, low)):
        ref[at, i * 128 : (i + 1) * 128] = part


def swap_sub(a, b, low):
    return jnp.where(low, a, pltpu.roll(b, 4, 0)), jnp.where(low, pltpu.roll(a, 4, 0), b)


def swap_lane(a, b, low):
    return jnp.where(low, a, pltpu.roll(b, 64, 1)), jnp.where(low, pltpu.roll(a, 64, 1), b)


def halves():
    sub = lax.broadcasted_iota(jnp.int32, (8, 128), 0) < 4
    lane = lax.broadcasted_iota(jnp.int32, (8, 128), 1)
    return sub, lane < 64, lane % 64


def forward_kernel(z_ref, dft_ref, tw_ref, own_ref, up_ref, dn_ref, x_ref, y_ref):
    for f in range(3):
        spec = real_fft([z_ref[d, :, f * 128 : (f + 1) * 128] for d in range(NB)])
        for k in range(NK):
            a, b = spec[k]
            c, s = tw_ref[k, 0:1, :], tw_ref[k, 1:2, :]
            if b is None:
                re, im = a * c, -(a * s)
            else:
                re, im = a * c + b * s, b * c - a * s
            split_store(x_ref, slice((f * NK + k) * 16, (f * NK + k) * 16 + 16), re, im)
    y_ref[...] = jnp.dot(x_ref[...], dft_ref[...], preferred_element_type=jnp.float32)
    sub, lane, inner = halves()
    for i in range(PAIRS):
        tiles = []
        for f in range(3):
            parts = []
            for k in (2 * i, 2 * i + 1):
                if k == NK:
                    parts.append((jnp.zeros((8, 128), jnp.float32),) * 2)
                    continue
                at = (f * NK + k) * 16
                re = y_ref[at : at + 8, :128] + y_ref[at + 8 : at + 16, 128:]
                im = y_ref[at + 8 : at + 16, :128] - y_ref[at : at + 8, 128:]
                parts.append(swap_sub(re, im, sub))
            rows = []
            for half in range(2):
                rows += swap_lane(parts[0][half], parts[1][half], lane)
            for j in range(ROWS):
                own_ref[(i * 3 + f) * ROWS + j] = rows[j]
            tiles.append(rows)
        u, v, h = tiles
        for ref, first in ((up_ref, 1), (dn_ref, 0)):
            main = v[first : first + 3] + h[first : first + 3]
            side = u[2:4] if first else u[0:2]
            for n in range(6):
                extra = pltpu.roll(side[n // 3], 48 - 16 * (n % 3), 1)
                ref[i * 6 + n] = jnp.where(inner < 48, main[n], extra)


def step_kernel(
    own_ref, up_ref, dn_ref, cut_ref, speed_ref, slope_ref, least_ref, band_ref, dft_ref, tw_ref,
    w_ref, x_ref, y_ref,
):
    z = lax.axis_index("lat")
    sub, lane, inner = halves()
    speed = speed_ref[...]
    turn_speed = jnp.where(sub, -speed, speed)
    half_speed = 0.5 * speed

    def body(i, carry):
        def received(ref):
            tiles = [ref[i * 6 + n] for n in range(6)]
            side = []
            for n in (0, 3):
                one, two, three = (pltpu.roll(tiles[n + c], 128 - 48 + 16 * c, 1) for c in range(3))
                side.append(jnp.where(inner < 16, one, jnp.where(inner < 32, two, three)))
            return side, tiles[:3], tiles[3:]

        above, below = received(up_ref), received(dn_ref)
        mine = [[own_ref[(i * 3 + f) * ROWS + j] for j in range(ROWS)] for f in range(3)]
        u = [None] + above[0] + mine[0] + below[0] + [None]
        v = above[1] + mine[1] + below[1]
        h = above[2] + mine[2] + below[2]
        start = (u, v, h)
        least = least_ref[i]
        wave = turn_speed * slope_ref[i]
        count = ROWS + 2 * HALO
        keep, zs = [None] * count, [None] * count
        for j in range(1, count - 1):
            keep[j] = jnp.where(least <= cut_ref[j : j + 1, :], 1.0, 0.0)
            zs[j] = wave * band_ref[z, 1, j : j + 1, :]

        def advance(state, margin, scale):
            su, sv, sh = state
            vc = [None] * count
            for j in range(margin - 1, count - margin + 1):
                vc[j] = sv[j] * band_ref[z, 2, j : j + 1, :]
            out = ([None] * count, [None] * count, [None] * count)
            for j in range(margin, count - margin):
                cor = band_ref[z, 0, j : j + 1, :]
                tu = cor * sv[j] - zs[j] * pltpu.roll(sh[j], 4, 0)
                tv = cor * su[j] + half_speed * (sh[j - 1] - sh[j + 1])
                th = zs[j] * pltpu.roll(su[j], 4, 0) + (speed * band_ref[z, 3, j : j + 1, :]) * (
                    vc[j - 1] - vc[j + 1]
                )
                if scale is None:
                    out[0][j], out[1][j], out[2][j] = keep[j] * tu, -keep[j] * tv, -keep[j] * th
                else:
                    m = keep[j] * scale
                    out[0][j] = u[j] + m * tu
                    out[1][j] = v[j] - m * tv
                    out[2][j] = h[j] - m * th
            return out

        gain = advance(advance(advance(start, 1, 1.0 / 3.0), 2, 0.5), 3, None)
        for f in range(3):
            rows = gain[f][HALO : HALO + ROWS]
            north, south = swap_lane(rows[0], rows[1], lane), swap_lane(rows[2], rows[3], lane)
            for side in range(2):
                re, im = swap_sub(north[side], south[side], sub)
                at = (f * 2 * PAIRS + side) * 16 + i * 32
                split_store(x_ref, pl.ds(at, 16), re, im)
        return carry

    for i in range(PAIRS):
        body(i, 0)
    y_ref[...] = jnp.dot(x_ref[...], dft_ref[...], preferred_element_type=jnp.float32)
    for f in range(3):
        spec = []
        for k in range(NK):
            at = (f * 2 * PAIRS + k) * 16
            a = y_ref[at : at + 8, :128] - y_ref[at + 8 : at + 16, 128:]
            b = y_ref[at + 8 : at + 16, :128] + y_ref[at : at + 8, 128:]
            c, s = tw_ref[k, 0:1, :], tw_ref[k, 1:2, :]
            spec.append((a * c - b * s, a * s + b * c))
        for d, value in enumerate(real_ifft(spec)):
            w_ref[d, :, f * 128 : (f + 1) * 128] = value


def unpack_kernel(w_ref, u_ref, v_ref, h_ref, u_hbm, v_hbm, h_hbm, out, sem):
    copies = []
    for f, (ref, hbm) in enumerate(((u_ref, u_hbm), (v_ref, v_hbm), (h_ref, h_hbm))):
        for half in range(2):
            block = [w_ref[:, half * LV + l, f * 128 : (f + 1) * 128] for l in range(LV)]
            turned = jnp.concatenate(block, axis=0).T
            for side in range(2):
                j = half * 2 + side
                out[f, :, j, :] = ref[:, j, :] + turned[side * 64 : side * 64 + NR, :]
        copies.append(pltpu.make_async_copy(out.at[f], hbm, sem.at[f]))
        copies[-1].start()
    for copy in copies:
        copy.wait()


def vmem(count):
    return [pl.BlockSpec(memory_space=pltpu.VMEM)] * count


def hbm(count):
    return [pl.BlockSpec(memory_space=pltpu.HBM)] * count


def shaped(*dims):
    return jax.ShapeDtypeStruct(dims, jnp.float32)


def shards(u_wind, v_wind, height, wave_speed, cutoff):
    bands = lax.axis_size("lat")
    dft, twid, twid_back, slope, least, per_band = host_tables(bands)
    levels = u_wind.shape[2]
    packed, cut_rows, speeds = pl.pallas_call(
        pack_kernel,
        out_shape=(
            shaped(NB, 2 * LV, 384),
            jax.ShapeDtypeStruct((16, 128), jnp.int32),
            shaped(8, 128),
        ),
        in_specs=hbm(5),
        out_specs=tuple(vmem(3)),
        scratch_shapes=[
            pltpu.VMEM((3, NR, ROWS, levels), jnp.float32),
            pltpu.VMEM((3, 2, 128, levels), jnp.float32),
            pltpu.SMEM(cutoff.shape, jnp.int32),
            pltpu.SMEM(wave_speed.shape, jnp.float32),
            pltpu.SemaphoreType.DMA((5,)),
        ],
        name="pack",
        compiler_params=PARAMS,
    )(*(pltpu.with_memory_space_constraint(a, pltpu.HBM) for a in (u_wind, v_wind, height, cutoff, wave_speed)))
    circles = lax.all_to_all(packed, LON, 0, 0, tiled=True)
    own, up, dn = pl.pallas_call(
        forward_kernel,
        out_shape=(
            shaped(PAIRS * 3 * ROWS, 8, 128),
            shaped(PAIRS * 6, 8, 128),
            shaped(PAIRS * 6, 8, 128),
        ),
        in_specs=vmem(3),
        out_specs=tuple(vmem(3)),
        scratch_shapes=[
            pltpu.VMEM((3 * NK * 16, 768), jnp.bfloat16),
            pltpu.VMEM((3 * NK * 16, 256), jnp.float32),
        ],
        name="forward",
        compiler_params=PARAMS,
    )(circles, dft, twid)
    south = [(i, i + 1) for i in range(bands - 1)]
    north = [(b, a) for a, b in south]
    up = lax.ppermute(up, "lat", south)
    dn = lax.ppermute(dn, "lat", north)
    waves = pl.pallas_call(
        step_kernel,
        out_shape=shaped(NB, 2 * LV, 384),
        in_specs=vmem(10),
        out_specs=vmem(1)[0],
        scratch_shapes=[
            pltpu.VMEM((3 * 2 * PAIRS * 16, 768), jnp.bfloat16),
            pltpu.VMEM((3 * 2 * PAIRS * 16, 256), jnp.float32),
        ],
        name="sections",
        compiler_params=PARAMS,
    )(own, up, dn, cut_rows, speeds, slope, least, per_band, dft, twid_back)
    waves = lax.all_to_all(waves, LON, 0, 0, tiled=True)
    return pl.pallas_call(
        unpack_kernel,
        out_shape=tuple(shaped(NR, ROWS, levels) for _ in range(3)),
        in_specs=vmem(4),
        out_specs=tuple(hbm(3)),
        scratch_shapes=[
            pltpu.VMEM((3, NR, ROWS, levels), jnp.float32),
            pltpu.SemaphoreType.DMA((3,)),
        ],
        name="unpack",
        compiler_params=PARAMS,
    )(waves, u_wind, v_wind, height)


def solution(mesh):
    split = Mesh(
        mesh.devices.reshape(mesh.shape["lat"], 4, 4, 2), ("lat", "lon_0", "lon_1", "lon_2")
    )
    return jax.shard_map(
        shards,
        mesh=split,
        in_specs=(P(LON, "lat", None), P(LON, "lat", None), P(LON, "lat", None), P(), P()),
        out_specs=(P(LON, "lat", None), P(LON, "lat", None), P(LON, "lat", None)),
        check_vma=False,
    )
```

profile of v0, /device:TPU:97, one launch (start us, length us, event | category | flops | bytes accessed | tf_op | source)
XLA Modules:
  0.0 52.3 jit_solution(9960266053303378307)
XLA Ops:
  0.6 1.5 %pack.1 = (f32[32,8,384]{2,1,0:T(8,128)S(1)}, s32[16,128]{1,0:T(8,128)S(1)}, f32[8,128]{1,0:T(8,128)S(1)}) custom-call(f32[45,4,128]{2,1,0:T(4,128)} %u_ref.1, f32[45,4,128]{2,1,0:T(4,128)} %v_ref.1, f32[45,4,128]{2,1,0:T(4,128)} %h_ref.1, s32[32]{0:T(128)} %cut_hbm.1, f32[128]{0:T(128)} %speed_hbm.1), custom_call_target="tpu_custom_call" | custom-call | tf_op jit(solution)/shard_map/pack/pallas_call | solution.py:352
  2.2 0.0 copy-start
  2.2 0.0 copy-start.5
  2.2 17.8 %all_to_all.10.z_ref = f32[32,8,384]{2,1,0:T(8,128)S(1)} all-to-all(f32[32,8,384]{2,1,0:T(8,128)S(1)} %get-tuple-element.9), channel_id=1, replica_groups=mesh['lat'=8,'lon_0'=4,'lon_1'=4,'lon_2'=2] {'lon_0','lon_1','lon_2'}, dimensions={0} | all-to-all | bytes 786432 | tf_op jit(solution)/shard_map/all_to_all | solution.py:371
  20.0 0.0 copy-done
  20.0 0.0 copy-done.5
  20.0 0.0 copy-start.4
  20.0 0.0 copy-start.6
  20.0 0.6 %forward.1 = (f32[108,8,128]{2,1,0:T(8,128)S(1)}, f32[54,8,128]{2,1,0:T(8,128)S(1)}, f32[54,8,128]{2,1,0:T(8,128)S(1)}) custom-call(f32[32,8,384]{2,1,0:T(8,128)S(1)} %all_to_all.10.z_ref, bf16[768,256]{1,0:T(8,128)(2,1)S(1)} %copy-done, f32[17,2,128]{2,1,0:T(2,128)S(1)} %copy-done.5), custom_call_target="tpu_custom_call" | custom-call | tf_op jit(solution)/shard_map/forward/pallas_call | solution.py:372
  20.7 0.0 copy-start.7
  20.7 0.0 copy-start.8
  20.7 4.8 %collective-permute-start = (f32[54,8,128]{2,1,0:T(8,128)S(1)}, f32[54,8,128]{2,1,0:T(8,128)S(1)}, u32[]{:S(2)}, u32[]{:S(2)}) collective-permute-start(f32[54,8,128]{2,1,0:T(8,128)S(1)} %get-tuple-element.11), channel_id=1, source_target_pairs={{0,32},{32,64},{64,96},{96,128},{128,160},{160,192},{192,224},{1,3... | collective-permute-start | bytes 663560 | tf_op jit(solution)/shard_map/ppermute | solution.py:390
  25.5 1.9 %collective-permute-start.1 = (f32[54,8,128]{2,1,0:T(8,128)S(1)}, f32[54,8,128]{2,1,0:T(8,128)S(1)}, u32[]{:S(2)}, u32[]{:S(2)}) collective-permute-start(f32[54,8,128]{2,1,0:T(8,128)S(1)} %get-tuple-element.12), channel_id=1, source_target_pairs={{32,0},{64,32},{96,64},{128,96},{160,128},{192,160},{224,192},{33,... | collective-permute-start | bytes 663560 | tf_op jit(solution)/shard_map/ppermute | solution.py:391
  27.4 2.6 %collective-permute-done.up_ref = f32[54,8,128]{2,1,0:T(8,128)S(1)} collective-permute-done((f32[54,8,128]{2,1,0:T(8,128)S(1)}, f32[54,8,128]{2,1,0:T(8,128)S(1)}, u32[]{:S(2)}, u32[]{:S(2)}) %collective-permute-start) | collective-permute-done | bytes 221216 | tf_op jit(solution)/shard_map/ppermute | solution.py:390
  29.9 5.0 %collective-permute-done.1.dn_ref = f32[54,8,128]{2,1,0:T(8,128)S(1)} collective-permute-done((f32[54,8,128]{2,1,0:T(8,128)S(1)}, f32[54,8,128]{2,1,0:T(8,128)S(1)}, u32[]{:S(2)}, u32[]{:S(2)}) %collective-permute-start.1) | collective-permute-done | bytes 221216 | tf_op jit(solution)/shard_map/ppermute | solution.py:391
  35.0 0.0 copy-done.4
  35.0 0.0 copy-done.6
  35.0 0.0 copy-done.7
  35.0 0.0 copy-done.8
  35.0 1.1 %sections.1 = f32[32,8,384]{2,1,0:T(8,128)S(1)} custom-call(f32[108,8,128]{2,1,0:T(8,128)S(1)} %get-tuple-element.10.own_ref, f32[54,8,128]{2,1,0:T(8,128)S(1)} %collective-permute-done.up_ref, f32[54,8,128]{2,1,0:T(8,128)S(1)} %collective-permute-done.1.dn_ref, s32[16,128]{1,0:T(8,128)S(1)} %get-tuple-element.13.cut_ref, ...), custom_call_target="tpu_custom_call" | custom-call | tf_op jit(solution)/shard_map/sections/pallas_call | solution.py:392
  36.1 0.0 copy-start.1
  36.1 0.0 copy-start.2
  36.1 0.0 copy-start.3
  36.1 15.1 %all_to_all.11.w_ref = f32[32,8,384]{2,1,0:T(8,128)S(1)} all-to-all(f32[32,8,384]{2,1,0:T(8,128)S(1)} %sections.1), channel_id=1, replica_groups=mesh['lat'=8,'lon_0'=4,'lon_1'=4,'lon_2'=2] {'lon_0','lon_1','lon_2'}, dimensions={0} | all-to-all | bytes 786432 | tf_op jit(solution)/shard_map/all_to_all | solution.py:404
  51.2 0.0 copy-done.1
  51.2 0.0 copy-done.2
  51.2 0.0 copy-done.3
  51.2 1.1 %unpack.1 = (f32[45,4,128]{2,1,0:T(4,128)}, f32[45,4,128]{2,1,0:T(4,128)}, f32[45,4,128]{2,1,0:T(4,128)}) custom-call(f32[32,8,384]{2,1,0:T(8,128)S(1)} %all_to_all.11.w_ref, f32[45,4,128]{2,1,0:T(4,128)S(1)} %copy-done.1, f32[45,4,128]{2,1,0:T(4,128)S(1)} %copy-done.2, f32[45,4,128]{2,1,0:T(4,128)S(1)} %copy-done.3), custom_call_target="tpu_custom_call" | custom-call | tf_op jit(solution)/shard_map/unpack/pallas_call | solution.py:405
Async XLA Ops:
  2.2 17.9 %copy-start = (bf16[768,256]{1,0:T(8,128)(2,1)S(1)}, bf16[768,256]{1,0:T(8,128)(2,1)}, u32[]{:S(2)}) copy-start(bf16[768,256]{1,0:T(8,128)(2,1)} %constant.12.clone.dft_ref) | copy-start | bytes 1179652
  2.2 17.9 %copy-start.5 = (f32[17,2,128]{2,1,0:T(2,128)S(1)}, f32[17,2,128]{2,1,0:T(2,128)}, u32[]{:S(2)}) copy-start(f32[17,2,128]{2,1,0:T(2,128)} %constant.13.clone.tw_ref) | copy-start | bytes 52228
  20.0 15.0 %copy-start.4 = (f32[8,4,16,128]{3,2,1,0:T(8,128)S(1)}, f32[8,4,16,128]{3,2,1,0:T(8,128)}, u32[]{:S(2)}) copy-start(f32[8,4,16,128]{3,2,1,0:T(8,128)} %constant.17.clone.band_ref) | copy-start | bytes 786436
  20.0 15.0 %copy-start.6 = (f32[17,2,128]{2,1,0:T(2,128)S(1)}, f32[17,2,128]{2,1,0:T(2,128)}, u32[]{:S(2)}) copy-start(f32[17,2,128]{2,1,0:T(2,128)} %constant.14.clone.tw_ref) | copy-start | bytes 52228
  20.7 14.3 %copy-start.7 = (s32[9,1,128]{2,1,0:T(1,128)S(1)}, s32[9,1,128]{2,1,0:T(1,128)}, u32[]{:S(2)}) copy-start(s32[9,1,128]{2,1,0:T(1,128)} %constant.16.clone.least_ref) | copy-start | bytes 13828
  20.7 14.3 %copy-start.8 = (f32[9,1,128]{2,1,0:T(1,128)S(1)}, f32[9,1,128]{2,1,0:T(1,128)}, u32[]{:S(2)}) copy-start(f32[9,1,128]{2,1,0:T(1,128)} %constant.15.clone.slope_ref) | copy-start | bytes 13828
  20.7 9.3 %collective-permute-start = (f32[54,8,128]{2,1,0:T(8,128)S(1)}, f32[54,8,128]{2,1,0:T(8,128)S(1)}, u32[]{:S(2)}, u32[]{:S(2)}) collective-permute-start(f32[54,8,128]{2,1,0:T(8,128)S(1)} %get-tuple-element.11), channel_id=1, source_target_pairs={{0,32},{32,64},{64,96},{96,128},{128,160},{160,192},{192,224},{1,3... | collective-permute-start | bytes 663560 | tf_op jit(solution)/shard_map/ppermute | solution.py:390
  25.5 9.5 %collective-permute-start.1 = (f32[54,8,128]{2,1,0:T(8,128)S(1)}, f32[54,8,128]{2,1,0:T(8,128)S(1)}, u32[]{:S(2)}, u32[]{:S(2)}) collective-permute-start(f32[54,8,128]{2,1,0:T(8,128)S(1)} %get-tuple-element.12), channel_id=1, source_target_pairs={{32,0},{64,32},{96,64},{128,96},{160,128},{192,160},{224,192},{33,... | collective-permute-start | bytes 663560 | tf_op jit(solution)/shard_map/ppermute | solution.py:391
  36.1 15.1 %copy-start.1 = (f32[45,4,128]{2,1,0:T(4,128)S(1)}, f32[45,4,128]{2,1,0:T(4,128)}, u32[]{:S(2)}) copy-start(f32[45,4,128]{2,1,0:T(4,128)} %u_ref.1) | copy-start | bytes 276484
  36.1 15.1 %copy-start.2 = (f32[45,4,128]{2,1,0:T(4,128)S(1)}, f32[45,4,128]{2,1,0:T(4,128)}, u32[]{:S(2)}) copy-start(f32[45,4,128]{2,1,0:T(4,128)} %v_ref.1) | copy-start | bytes 276484
  36.1 15.1 %copy-start.3 = (f32[45,4,128]{2,1,0:T(4,128)S(1)}, f32[45,4,128]{2,1,0:T(4,128)}, u32[]{:S(2)}) copy-start(f32[45,4,128]{2,1,0:T(4,128)} %h_ref.1) | copy-start | bytes 276484
where the time goes:
time: 52.6 us; the launch traced here: 52.3 us
  blocking collectives  32.9 us (63%)
  waiting for transfers between devices  7.6 us (14%)
  starting transfers between devices  6.68 us (13%)
  Pallas kernels  4.29 us (8%)
  between operations  0.75 us (1%)
    all_to_all x1, blocking collectives, shards(): circles = lax.all_to_all(packed, LON, 0, 0, tiled=True)  17.8 us
    all_to_all x1, blocking collectives, shards(): waves = lax.all_to_all(waves, LON, 0, 0, tiled=True)  15.1 us
    ppermute x1, waiting for transfers between devices, shards(): dn = lax.ppermute(dn, 'lat', north)  5.05 us
    ppermute x1, starting transfers between devices, shards(): up = lax.ppermute(up, 'lat', south)  4.76 us
    ppermute x1, waiting for transfers between devices, shards(): up = lax.ppermute(up, 'lat', south)  2.56 us
    ppermute x1, starting transfers between devices, shards(): dn = lax.ppermute(dn, 'lat', north)  1.92 us
    pallas_call x1, Pallas kernels, shards(): pl.pallas_call(pack_kernel, out_shape=(shaped(NB, 2 * LV, 384), jax.Shape...  1.52 us
    pallas_call x1, Pallas kernels, shards(): pl.pallas_call(unpack_kernel, out_shape=tuple((shaped(NR, ROWS, levels) f...  1.1 us
  transfers between devices with their start and end apart: 2, of which 2 were waited for; matrix products, arithmetic and copies ran while one was open for 0% of the time, Pallas kernels for 0%

commit v1 on v0

--- a/solution.py
+++ b/solution.py
@@ -20,6 +20,7 @@
 ROWS = 4
 HALO = 3
 LV = 4
+SLOTS = 5
 FAR = 1 << 20
 PARAMS = pltpu.CompilerParams(vmem_limit_bytes=12 << 20)
 
@@ -147,14 +148,22 @@
     for copy in copies:
         copy.start()
     tmp[...] = jnp.zeros_like(tmp)
-    for f in range(3):
+    inner = lax.broadcasted_iota(jnp.int32, (128, 128), 1) % 64
+    extra = None
+    for f in (2, 0, 1):
         copies[f].wait()
         for j in range(ROWS):
             tmp[f, j // 2, j % 2 * 64 : j % 2 * 64 + NR, :] = raw[f, :, j, :]
-        for half in range(2):
+        for half in (1, 0):
+            n = 2 * f + half
             turned = tmp[f, half].T
+            if n == SLOTS:
+                extra = turned
+                continue
+            if n < 3:
+                turned = jnp.where(inner < 48, turned, spare_roll(extra, n))
             for l in range(LV):
-                o_ref[:, half * LV + l, f * 128 : (f + 1) * 128] = turned[l * NB : (l + 1) * NB, :]
+                o_ref[:, n, l, :] = turned[l * NB : (l + 1) * NB, :]
     copies[3].wait()
     copies[4].wait()
     z = lax.axis_index("lat")
@@ -174,6 +183,15 @@
     speed_ref[...] = value
 
 
+def spare_roll(a, n):
+    return pltpu.roll(a, 48 - 16 * n, 1)
+
+
+def from_spare(tiles, inner):
+    one, two, three = (pltpu.roll(t, 128 - 48 + 16 * n, 1) for n, t in enumerate(tiles))
+    return jnp.where(inner < 16, one, jnp.where(inner < 32, two, three))
+
+
 def split_store(ref, at, re, im):
     x = jnp.concatenate([re, im], axis=0)
     high = x.astype(jnp.bfloat16)
@@ -198,9 +216,20 @@
     return sub, lane < 64, lane % 64
 
 
-def forward_kernel(z_ref, dft_ref, tw_ref, own_ref, up_ref, dn_ref, x_ref, y_ref):
+def forward_kernel(z_ref, dft_ref, tw_ref, own_ref, one_ref, two_ref, x_ref, y_ref):
+    even = lax.axis_index("lon_2") == 0
+    sub, lane, inner = halves()
+    inner4 = lax.broadcasted_iota(jnp.int32, (LV, 128), 1) % 64
+
+    def slot(d, n):
+        if n < SLOTS:
+            return z_ref[d, n]
+        return from_spare([z_ref[d, i] for i in range(3)], inner4)
+
     for f in range(3):
-        spec = real_fft([z_ref[d, :, f * 128 : (f + 1) * 128] for d in range(NB)])
+        spec = real_fft(
+            [jnp.concatenate([slot(d, 2 * f), slot(d, 2 * f + 1)], axis=0) for d in range(NB)]
+        )
         for k in range(NK):
             a, b = spec[k]
             c, s = tw_ref[k, 0:1, :], tw_ref[k, 1:2, :]
@@ -210,7 +239,6 @@
                 re, im = a * c + b * s, b * c - a * s
             split_store(x_ref, slice((f * NK + k) * 16, (f * NK + k) * 16 + 16), re, im)
     y_ref[...] = jnp.dot(x_ref[...], dft_ref[...], preferred_element_type=jnp.float32)
-    sub, lane, inner = halves()
     for i in range(PAIRS):
         tiles = []
         for f in range(3):
@@ -230,34 +258,36 @@
                 own_ref[(i * 3 + f) * ROWS + j] = rows[j]
             tiles.append(rows)
         u, v, h = tiles
-        for ref, first in ((up_ref, 1), (dn_ref, 0)):
+        edges = []
+        for first in (1, 0):
             main = v[first : first + 3] + h[first : first + 3]
             side = u[2:4] if first else u[0:2]
-            for n in range(6):
-                extra = pltpu.roll(side[n // 3], 48 - 16 * (n % 3), 1)
-                ref[i * 6 + n] = jnp.where(inner < 48, main[n], extra)
+            edges.append(
+                [jnp.where(inner < 48, main[n], spare_roll(side[n // 3], n % 3)) for n in range(6)]
+            )
+        for n, (south, north) in enumerate(zip(*edges)):
+            one_ref[i * 6 + n] = jnp.where(even, south, north)
+            two_ref[i * 6 + n] = jnp.where(even, north, south)
 
 
 def step_kernel(
-    own_ref, up_ref, dn_ref, cut_ref, speed_ref, slope_ref, least_ref, band_ref, dft_ref, tw_ref,
-    w_ref, x_ref, y_ref,
+    own_ref, one_ref, two_ref, cut_ref, speed_ref, slope_ref, least_ref, band_ref, dft_ref, tw_ref,
+    w_ref, x_ref, y_ref, hold_ref,
 ):
     z = lax.axis_index("lat")
+    even = lax.axis_index("lon_2") == 0
     sub, lane, inner = halves()
     speed = speed_ref[...]
     turn_speed = jnp.where(sub, -speed, speed)
     half_speed = 0.5 * speed
 
     def body(i, carry):
-        def received(ref):
-            tiles = [ref[i * 6 + n] for n in range(6)]
-            side = []
-            for n in (0, 3):
-                one, two, three = (pltpu.roll(tiles[n + c], 128 - 48 + 16 * c, 1) for c in range(3))
-                side.append(jnp.where(inner < 16, one, jnp.where(inner < 32, two, three)))
+        def received(a_ref, b_ref):
+            tiles = [jnp.where(even, a_ref[i * 6 + n], b_ref[i * 6 + n]) for n in range(6)]
+            side = [from_spare(tiles[n : n + 3], inner) for n in (0, 3)]
             return side, tiles[:3], tiles[3:]
 
-        above, below = received(up_ref), received(dn_ref)
+        above, below = received(one_ref, two_ref), received(two_ref, one_ref)
         mine = [[own_ref[(i * 3 + f) * ROWS + j] for j in range(ROWS)] for f in range(3)]
         u = [None] + above[0] + mine[0] + below[0] + [None]
         v = above[1] + mine[1] + below[1]
@@ -306,7 +336,7 @@
     for i in range(PAIRS):
         body(i, 0)
     y_ref[...] = jnp.dot(x_ref[...], dft_ref[...], preferred_element_type=jnp.float32)
-    for f in range(3):
+    for f in (2, 0, 1):
         spec = []
         for k in range(NK):
             at = (f * 2 * PAIRS + k) * 16
@@ -315,15 +345,34 @@
             c, s = tw_ref[k, 0:1, :], tw_ref[k, 1:2, :]
             spec.append((a * c - b * s, a * s + b * c))
         for d, value in enumerate(real_ifft(spec)):
-            w_ref[d, :, f * 128 : (f + 1) * 128] = value
+            if f == 2:
+                w_ref[d, 4] = value[:LV]
+                low = pltpu.roll(value, LV, 0)
+                hold_ref[d] = jnp.where(sub, low, value)
+                continue
+            extra = hold_ref[d]
+            if f == 0:
+                extra = jnp.where(sub, spare_roll(extra, 0), spare_roll(extra, 1))
+                value = jnp.where(inner < 48, value, extra)
+            else:
+                extra = spare_roll(extra, 2)
+                value = jnp.where(jnp.logical_and(sub, inner >= 48), extra, value)
+            w_ref[d, 2 * f] = value[:LV]
+            w_ref[d, 2 * f + 1] = value[LV:]
 
 
 def unpack_kernel(w_ref, u_ref, v_ref, h_ref, u_hbm, v_hbm, h_hbm, out, sem):
     copies = []
+    inner = lax.broadcasted_iota(jnp.int32, (128, 128), 1) % 64
+
+    def slot(n):
+        if n == SLOTS:
+            return from_spare([slot(i) for i in range(3)], inner)
+        return jnp.concatenate([w_ref[:, n, l, :] for l in range(LV)], axis=0)
+
     for f, (ref, hbm) in enumerate(((u_ref, u_hbm), (v_ref, v_hbm), (h_ref, h_hbm))):
         for half in range(2):
-            block = [w_ref[:, half * LV + l, f * 128 : (f + 1) * 128] for l in range(LV)]
-            turned = jnp.concatenate(block, axis=0).T
+            turned = slot(2 * f + half).T
             for side in range(2):
                 j = half * 2 + side
                 out[f, :, j, :] = ref[:, j, :] + turned[side * 64 : side * 64 + NR, :]
@@ -352,7 +401,7 @@
     packed, cut_rows, speeds = pl.pallas_call(
         pack_kernel,
         out_shape=(
-            shaped(NB, 2 * LV, 384),
+            shaped(NB, SLOTS, LV, 128),
             jax.ShapeDtypeStruct((16, 128), jnp.int32),
             shaped(8, 128),
         ),
@@ -369,7 +418,7 @@
         compiler_params=PARAMS,
     )(*(pltpu.with_memory_space_constraint(a, pltpu.HBM) for a in (u_wind, v_wind, height, cutoff, wave_speed)))
     circles = lax.all_to_all(packed, LON, 0, 0, tiled=True)
-    own, up, dn = pl.pallas_call(
+    own, one, two = pl.pallas_call(
         forward_kernel,
         out_shape=(
             shaped(PAIRS * 3 * ROWS, 8, 128),
@@ -385,22 +434,24 @@
         name="forward",
         compiler_params=PARAMS,
     )(circles, dft, twid)
-    south = [(i, i + 1) for i in range(bands - 1)]
-    north = [(b, a) for a, b in south]
-    up = lax.ppermute(up, "lat", south)
-    dn = lax.ppermute(dn, "lat", north)
+    stop = bands - 1
+    south = [[(2 * i + c, 2 * i + 2 + c) for i in range(stop)] for c in range(2)]
+    north = [[(b, a) for a, b in pairs] for pairs in south]
+    one = lax.ppermute(one, ("lat", "lon_2"), south[0] + north[1])
+    two = lax.ppermute(two, ("lat", "lon_2"), north[0] + south[1])
     waves = pl.pallas_call(
         step_kernel,
-        out_shape=shaped(NB, 2 * LV, 384),
+        out_shape=shaped(NB, SLOTS, LV, 128),
         in_specs=vmem(10),
         out_specs=vmem(1)[0],
         scratch_shapes=[
             pltpu.VMEM((3 * 2 * PAIRS * 16, 768), jnp.bfloat16),
             pltpu.VMEM((3 * 2 * PAIRS * 16, 256), jnp.float32),
+            pltpu.VMEM((NB, 2 * LV, 128), jnp.float32),
         ],
         name="sections",
         compiler_params=PARAMS,
-    )(own, up, dn, cut_rows, speeds, slope, least, per_band, dft, twid_back)
+    )(own, one, two, cut_rows, speeds, slope, least, per_band, dft, twid_back)
     waves = lax.all_to_all(waves, LON, 0, 0, tiled=True)
     return pl.pallas_call(
         unpack_kernel,

time: 52.6 us -> 50.2 us (0.954)
  waiting for transfers between devices: 7.6 us -> 3.97 us
  blocking collectives: 32.9 us -> 33.8 us
    ppermute x2, waiting for transfers between devices: 7.6 us -> 3.97 us  [the longest x1 2.59 us: shards(): two = lax.ppermute(two, ('lat', 'lon_2'), north[0] + south[1])]
    all_to_all x1, blocking collectives: 15.1 us -> 16.6 us  [shards(): waves = lax.all_to_all(waves, LON, 0, 0, tiled=True)]
    all_to_all x1, blocking collectives: 17.8 us -> 17.2 us  [shards(): circles = lax.all_to_all(packed, LON, 0, 0, tiled=True)]
where the time goes in v1:
time: 50.2 us; the launch traced here: 49.9 us
  blocking collectives  33.8 us (67%)
  starting transfers between devices  6.68 us (13%)
  Pallas kernels  4.68 us (9%)
  waiting for transfers between devices  3.97 us (8%)
  between operations  0.74 us (1%)
    all_to_all x1, blocking collectives, shards(): circles = lax.all_to_all(packed, LON, 0, 0, tiled=True)  17.2 us
    all_to_all x1, blocking collectives, shards(): waves = lax.all_to_all(waves, LON, 0, 0, tiled=True)  16.6 us
    ppermute x1, starting transfers between devices, shards(): two = lax.ppermute(two, ('lat', 'lon_2'), north[0] + south[1])  4.76 us
    ppermute x1, waiting for transfers between devices, shards(): two = lax.ppermute(two, ('lat', 'lon_2'), north[0] + south[1])  2.59 us
    ppermute x1, starting transfers between devices, shards(): one = lax.ppermute(one, ('lat', 'lon_2'), south[0] + north[1])  1.92 us
    pallas_call x1, Pallas kernels, shards(): pl.pallas_call(pack_kernel, out_shape=(shaped(NB, SLOTS, LV, 128), jax.Sh...  1.57 us
    ppermute x1, waiting for transfers between devices, shards(): one = lax.ppermute(one, ('lat', 'lon_2'), south[0] + north[1])  1.38 us
    pallas_call x1, Pallas kernels, shards(): pl.pallas_call(unpack_kernel, out_shape=tuple((shaped(NR, ROWS, levels) f...  1.24 us
  transfers between devices with their start and end apart: 2, of which 2 were waited for; matrix products, arithmetic and copies ran while one was open for 0% of the time, Pallas kernels for 0%

profile of v1, /device:TPU:97, one launch (start us, length us, event | category | flops | bytes accessed | tf_op | source)
XLA Modules:
  0.0 49.9 jit_solution(3607067265013535693)
XLA Ops:
  0.6 1.6 %pack.1 = (f32[32,5,4,128]{3,2,1,0:T(4,128)S(1)}, s32[16,128]{1,0:T(8,128)S(1)}, f32[8,128]{1,0:T(8,128)S(1)}) custom-call(f32[45,4,128]{2,1,0:T(4,128)} %u_ref.1, f32[45,4,128]{2,1,0:T(4,128)} %v_ref.1, f32[45,4,128]{2,1,0:T(4,128)} %h_ref.1, s32[32]{0:T(128)} %cut_hbm.1, f32[128]{0:T(128)} %speed_hbm.1), custom_call_target="tpu_custom_call" | custom-call | tf_op jit(solution)/shard_map/pack/pallas_call | solution.py:401
  2.2 0.0 copy-start
  2.2 0.0 copy-start.5
  2.2 17.2 %all_to_all.10.z_ref = f32[32,5,4,128]{3,2,1,0:T(4,128)S(1)} all-to-all(f32[32,5,4,128]{3,2,1,0:T(4,128)S(1)} %get-tuple-element.9), channel_id=1, replica_groups=mesh['lat'=8,'lon_0'=4,'lon_1'=4,'lon_2'=2] {'lon_0','lon_1','lon_2'}, dimensions={0} | all-to-all | bytes 655360 | tf_op jit(solution)/shard_map/all_to_all | solution.py:420
  19.4 0.0 copy-done
  19.4 0.0 copy-done.5
  19.4 0.0 copy-start.4
  19.4 0.0 copy-start.6
  19.5 0.7 %forward.1 = (f32[108,8,128]{2,1,0:T(8,128)S(1)}, f32[54,8,128]{2,1,0:T(8,128)S(1)}, f32[54,8,128]{2,1,0:T(8,128)S(1)}) custom-call(f32[32,5,4,128]{3,2,1,0:T(4,128)S(1)} %all_to_all.10.z_ref, bf16[768,256]{1,0:T(8,128)(2,1)S(1)} %copy-done, f32[17,2,128]{2,1,0:T(2,128)S(1)} %copy-done.5), custom_call_target="tpu_custom_call" | custom-call | tf_op jit(solution)/shard_map/forward/pallas_call | solution.py:421
  20.1 0.0 copy-start.7
  20.1 0.0 copy-start.8
  20.2 1.9 %collective-permute-start = (f32[54,8,128]{2,1,0:T(8,128)S(1)}, f32[54,8,128]{2,1,0:T(8,128)S(1)}, u32[]{:S(2)}, u32[]{:S(2)}) collective-permute-start(f32[54,8,128]{2,1,0:T(8,128)S(1)} %get-tuple-element.11), channel_id=1, source_target_pairs={{0,32},{32,64},{64,96},{96,128},{128,160},{160,192},{192,224},{33,... | collective-permute-start | bytes 663560 | tf_op jit(solution)/shard_map/ppermute | solution.py:440
  22.1 4.8 %collective-permute-start.1 = (f32[54,8,128]{2,1,0:T(8,128)S(1)}, f32[54,8,128]{2,1,0:T(8,128)S(1)}, u32[]{:S(2)}, u32[]{:S(2)}) collective-permute-start(f32[54,8,128]{2,1,0:T(8,128)S(1)} %get-tuple-element.12), channel_id=1, source_target_pairs={{32,0},{64,32},{96,64},{128,96},{160,128},{192,160},{224,192},{1,3... | collective-permute-start | bytes 663560 | tf_op jit(solution)/shard_map/ppermute | solution.py:441
  26.9 1.4 %collective-permute-done.one_ref = f32[54,8,128]{2,1,0:T(8,128)S(1)} collective-permute-done((f32[54,8,128]{2,1,0:T(8,128)S(1)}, f32[54,8,128]{2,1,0:T(8,128)S(1)}, u32[]{:S(2)}, u32[]{:S(2)}) %collective-permute-start) | collective-permute-done | bytes 221216 | tf_op jit(solution)/shard_map/ppermute | solution.py:440
  28.2 2.6 %collective-permute-done.1.two_ref = f32[54,8,128]{2,1,0:T(8,128)S(1)} collective-permute-done((f32[54,8,128]{2,1,0:T(8,128)S(1)}, f32[54,8,128]{2,1,0:T(8,128)S(1)}, u32[]{:S(2)}, u32[]{:S(2)}) %collective-permute-start.1) | collective-permute-done | bytes 221216 | tf_op jit(solution)/shard_map/ppermute | solution.py:441
  30.8 0.0 copy-done.4
  30.8 0.0 copy-done.6
  30.8 0.0 copy-done.7
  30.8 0.0 copy-done.8
  30.8 1.2 %sections.1 = f32[32,5,4,128]{3,2,1,0:T(4,128)S(1)} custom-call(f32[108,8,128]{2,1,0:T(8,128)S(1)} %get-tuple-element.10.own_ref, f32[54,8,128]{2,1,0:T(8,128)S(1)} %collective-permute-done.one_ref, f32[54,8,128]{2,1,0:T(8,128)S(1)} %collective-permute-done.1.two_ref, s32[16,128]{1,0:T(8,128)S(1)} %get-tuple-element.13.cut_ref, ...), custom_call_target="tpu_custom_call" | custom-call | tf_op jit(solution)/shard_map/sections/pallas_call | solution.py:442
  32.0 0.0 copy-start.1
  32.0 0.0 copy-start.2
  32.1 0.0 copy-start.3
  32.1 16.6 %all_to_all.11.w_ref = f32[32,5,4,128]{3,2,1,0:T(4,128)S(1)} all-to-all(f32[32,5,4,128]{3,2,1,0:T(4,128)S(1)} %sections.1), channel_id=1, replica_groups=mesh['lat'=8,'lon_0'=4,'lon_1'=4,'lon_2'=2] {'lon_0','lon_1','lon_2'}, dimensions={0} | all-to-all | bytes 655360 | tf_op jit(solution)/shard_map/all_to_all | solution.py:455
  48.7 0.0 copy-done.1
  48.7 0.0 copy-done.2
  48.7 0.0 copy-done.3
  48.7 1.2 %unpack.1 = (f32[45,4,128]{2,1,0:T(4,128)}, f32[45,4,128]{2,1,0:T(4,128)}, f32[45,4,128]{2,1,0:T(4,128)}) custom-call(f32[32,5,4,128]{3,2,1,0:T(4,128)S(1)} %all_to_all.11.w_ref, f32[45,4,128]{2,1,0:T(4,128)S(1)} %copy-done.1, f32[45,4,128]{2,1,0:T(4,128)S(1)} %copy-done.2, f32[45,4,128]{2,1,0:T(4,128)S(1)} %copy-done.3), custom_call_target="tpu_custom_call" | custom-call | tf_op jit(solution)/shard_map/unpack/pallas_call | solution.py:456
Async XLA Ops:
  2.2 17.2 %copy-start = (bf16[768,256]{1,0:T(8,128)(2,1)S(1)}, bf16[768,256]{1,0:T(8,128)(2,1)}, u32[]{:S(2)}) copy-start(bf16[768,256]{1,0:T(8,128)(2,1)} %constant.12.clone.dft_ref) | copy-start | bytes 1179652
  2.2 17.2 %copy-start.5 = (f32[17,2,128]{2,1,0:T(2,128)S(1)}, f32[17,2,128]{2,1,0:T(2,128)}, u32[]{:S(2)}) copy-start(f32[17,2,128]{2,1,0:T(2,128)} %constant.13.clone.tw_ref) | copy-start | bytes 52228
  19.4 11.4 %copy-start.4 = (f32[8,4,16,128]{3,2,1,0:T(8,128)S(1)}, f32[8,4,16,128]{3,2,1,0:T(8,128)}, u32[]{:S(2)}) copy-start(f32[8,4,16,128]{3,2,1,0:T(8,128)} %constant.17.clone.band_ref) | copy-start | bytes 786436
  19.4 11.4 %copy-start.6 = (f32[17,2,128]{2,1,0:T(2,128)S(1)}, f32[17,2,128]{2,1,0:T(2,128)}, u32[]{:S(2)}) copy-start(f32[17,2,128]{2,1,0:T(2,128)} %constant.14.clone.tw_ref) | copy-start | bytes 52228
  20.1 10.7 %copy-start.7 = (s32[9,1,128]{2,1,0:T(1,128)S(1)}, s32[9,1,128]{2,1,0:T(1,128)}, u32[]{:S(2)}) copy-start(s32[9,1,128]{2,1,0:T(1,128)} %constant.16.clone.least_ref) | copy-start | bytes 13828
  20.1 10.7 %copy-start.8 = (f32[9,1,128]{2,1,0:T(1,128)S(1)}, f32[9,1,128]{2,1,0:T(1,128)}, u32[]{:S(2)}) copy-start(f32[9,1,128]{2,1,0:T(1,128)} %constant.15.clone.slope_ref) | copy-start | bytes 13828
  20.2 8.1 %collective-permute-start = (f32[54,8,128]{2,1,0:T(8,128)S(1)}, f32[54,8,128]{2,1,0:T(8,128)S(1)}, u32[]{:S(2)}, u32[]{:S(2)}) collective-permute-start(f32[54,8,128]{2,1,0:T(8,128)S(1)} %get-tuple-element.11), channel_id=1, source_target_pairs={{0,32},{32,64},{64,96},{96,128},{128,160},{160,192},{192,224},{33,... | collective-permute-start | bytes 663560 | tf_op jit(solution)/shard_map/ppermute | solution.py:440
  22.1 8.7 %collective-permute-start.1 = (f32[54,8,128]{2,1,0:T(8,128)S(1)}, f32[54,8,128]{2,1,0:T(8,128)S(1)}, u32[]{:S(2)}, u32[]{:S(2)}) collective-permute-start(f32[54,8,128]{2,1,0:T(8,128)S(1)} %get-tuple-element.12), channel_id=1, source_target_pairs={{32,0},{64,32},{96,64},{128,96},{160,128},{192,160},{224,192},{1,3... | collective-permute-start | bytes 663560 | tf_op jit(solution)/shard_map/ppermute | solution.py:441
  32.0 16.6 %copy-start.1 = (f32[45,4,128]{2,1,0:T(4,128)S(1)}, f32[45,4,128]{2,1,0:T(4,128)}, u32[]{:S(2)}) copy-start(f32[45,4,128]{2,1,0:T(4,128)} %u_ref.1) | copy-start | bytes 276484
  32.0 16.6 %copy-start.2 = (f32[45,4,128]{2,1,0:T(4,128)S(1)}, f32[45,4,128]{2,1,0:T(4,128)}, u32[]{:S(2)}) copy-start(f32[45,4,128]{2,1,0:T(4,128)} %v_ref.1) | copy-start | bytes 276484
  32.1 16.6 %copy-start.3 = (f32[45,4,128]{2,1,0:T(4,128)S(1)}, f32[45,4,128]{2,1,0:T(4,128)}, u32[]{:S(2)}) copy-start(f32[45,4,128]{2,1,0:T(4,128)} %h_ref.1) | copy-start | bytes 276484

commit v2 on v1

--- a/solution.py
+++ b/solution.py
@@ -21,6 +21,7 @@
 HALO = 3
 LV = 4
 SLOTS = 5
+SENT = 41
 FAR = 1 << 20
 PARAMS = pltpu.CompilerParams(vmem_limit_bytes=12 << 20)
 
@@ -139,19 +140,21 @@
 
 
 def pack_kernel(u_hbm, v_hbm, h_hbm, cut_hbm, speed_hbm, o_ref, cut_ref, speed_ref, raw, tmp, cut, speed, sem):
-    copies = [
+    fields = [
         pltpu.make_async_copy(src, raw.at[f], sem.at[f])
-        for f, src in enumerate((u_hbm, v_hbm, h_hbm))
+        for f, src in ((2, h_hbm), (0, u_hbm), (1, v_hbm))
     ]
-    copies.append(pltpu.make_async_copy(cut_hbm, cut, sem.at[3]))
-    copies.append(pltpu.make_async_copy(speed_hbm, speed, sem.at[4]))
-    for copy in copies:
+    small = [
+        pltpu.make_async_copy(cut_hbm, cut, sem.at[3]),
+        pltpu.make_async_copy(speed_hbm, speed, sem.at[4]),
+    ]
+    for copy in fields + small:
         copy.start()
     tmp[...] = jnp.zeros_like(tmp)
     inner = lax.broadcasted_iota(jnp.int32, (128, 128), 1) % 64
     extra = None
-    for f in (2, 0, 1):
-        copies[f].wait()
+    for f, copy in zip((2, 0, 1), fields):
+        copy.wait()
         for j in range(ROWS):
             tmp[f, j // 2, j % 2 * 64 : j % 2 * 64 + NR, :] = raw[f, :, j, :]
         for half in (1, 0):
@@ -164,8 +167,8 @@
                 turned = jnp.where(inner < 48, turned, spare_roll(extra, n))
             for l in range(LV):
                 o_ref[:, n, l, :] = turned[l * NB : (l + 1) * NB, :]
-    copies[3].wait()
-    copies[4].wait()
+    for copy in small:
+        copy.wait()
     z = lax.axis_index("lat")
     p = (lax.axis_index("lon_0") * 4 + lax.axis_index("lon_1")) * 2 + lax.axis_index("lon_2")
     total = cut.shape[0]
@@ -216,7 +219,65 @@
     return sub, lane < 64, lane % 64
 
 
-def forward_kernel(z_ref, dft_ref, tw_ref, own_ref, one_ref, two_ref, x_ref, y_ref):
+class Rows:
+    def __init__(self, z, i, cut_ref, speed, turn_speed, slope_ref, least_ref, band_ref):
+        self.z, self.cut, self.band, self.speed = z, cut_ref, band_ref, speed
+        self.least, self.wave = least_ref[i], turn_speed * slope_ref[i]
+
+    def of(self, c, row):
+        return self.band[self.z, c, row + HALO : row + HALO + 1, :]
+
+    def keep(self, row):
+        kept = self.least <= self.cut[row + HALO : row + HALO + 1, :]
+        return jnp.where(kept, 1.0, 0.0)
+
+    def cor(self, row):
+        return self.of(0, row)
+
+    def zonal(self, row):
+        return self.wave * self.of(1, row)
+
+    def cos(self, row):
+        return self.of(2, row)
+
+    def merid(self, row):
+        return self.speed * self.of(3, row)
+
+
+def swap_parts(a):
+    return pltpu.roll(a, LV, 0)
+
+
+def edge_sums(u, v, h, rows, half_speed, edge, step):
+    near, far = edge + step, edge + 2 * step
+    sign = -1.0 if step > 0 else 1.0
+    keep, cor, zonal = rows.keep(edge), rows.cor(edge), rows.zonal(edge)
+    third, half = keep * (1.0 / 3.0), keep * 0.5
+    hs, merid = sign * half_speed, sign * rows.merid(edge)
+    vc_edge, vc_near, vc_far = (v[j] * rows.cos(j) for j in (edge, near, far))
+    v1 = v[edge] - third * (cor * u[edge] + hs * h[near])
+    h1 = h[edge] - third * (zonal * swap_parts(u[edge]) + merid * vc_near)
+    u1 = u[edge] + third * (cor * v[edge] - zonal * swap_parts(h[edge]))
+    near_third = rows.keep(near) * (1.0 / 3.0)
+    near_v1 = v[near] - near_third * (rows.cor(near) * u[near] + hs * (h[far] - h[edge]))
+    near_h1 = h[near] - near_third * (
+        rows.zonal(near) * swap_parts(u[near]) + sign * rows.merid(near) * (vc_far - vc_edge)
+    )
+    v2 = v[edge] - half * (cor * u1 + hs * near_h1)
+    h2 = h[edge] - half * (zonal * swap_parts(u1) + merid * (near_v1 * rows.cos(near)))
+    return [v[edge], h[edge], v1, h1, v2, h2]
+
+
+def field_dot(y_ref, x_ref, dft_ref, f, count):
+    at = slice(f * count * 16, (f + 1) * count * 16)
+    y_ref[at, :] = jnp.dot(x_ref[at, :], dft_ref[...], preferred_element_type=jnp.float32)
+
+
+def forward_kernel(
+    z_ref, dft_ref, tw_ref, cut_ref, speed_ref, slope_ref, least_ref, band_ref,
+    own_ref, one_ref, two_ref, x_ref, y_ref,
+):
+    z = lax.axis_index("lat")
     even = lax.axis_index("lon_2") == 0
     sub, lane, inner = halves()
     inner4 = lax.broadcasted_iota(jnp.int32, (LV, 128), 1) % 64
@@ -238,8 +299,12 @@
             else:
                 re, im = a * c + b * s, b * c - a * s
             split_store(x_ref, slice((f * NK + k) * 16, (f * NK + k) * 16 + 16), re, im)
-    y_ref[...] = jnp.dot(x_ref[...], dft_ref[...], preferred_element_type=jnp.float32)
-    for i in range(PAIRS):
+        field_dot(y_ref, x_ref, dft_ref, f, NK)
+    speed = speed_ref[...]
+    turn_speed = jnp.where(sub, -speed, speed)
+    half_speed = 0.5 * speed
+    spare = {}
+    for i in reversed(range(PAIRS)):
         tiles = []
         for f in range(3):
             parts = []
@@ -258,16 +323,22 @@
                 own_ref[(i * 3 + f) * ROWS + j] = rows[j]
             tiles.append(rows)
         u, v, h = tiles
-        edges = []
-        for first in (1, 0):
-            main = v[first : first + 3] + h[first : first + 3]
-            side = u[2:4] if first else u[0:2]
-            edges.append(
-                [jnp.where(inner < 48, main[n], spare_roll(side[n // 3], n % 3)) for n in range(6)]
-            )
-        for n, (south, north) in enumerate(zip(*edges)):
-            one_ref[i * 6 + n] = jnp.where(even, south, north)
-            two_ref[i * 6 + n] = jnp.where(even, north, south)
+        rows = Rows(z, i, cut_ref, speed, turn_speed, slope_ref, least_ref, band_ref)
+        to_south = edge_sums(u, v, h, rows, half_speed, ROWS - 1, -1)
+        to_north = edge_sums(u, v, h, rows, half_speed, 0, 1)
+        for n, (south, north) in enumerate(zip(to_south, to_north)):
+            t = i * 6 + n
+            for ref, tile in (
+                (one_ref, jnp.where(even, south, north)),
+                (two_ref, jnp.where(even, north, south)),
+            ):
+                if t >= SENT:
+                    spare[ref is one_ref, t - SENT] = tile
+                elif t < 3 * (PAIRS * 6 - SENT):
+                    extra = spare_roll(spare[ref is one_ref, t // 3], t % 3)
+                    ref[t] = jnp.where(inner < 48, tile, extra)
+                else:
+                    ref[t] = tile
 
 
 def step_kernel(
@@ -281,62 +352,64 @@
     turn_speed = jnp.where(sub, -speed, speed)
     half_speed = 0.5 * speed
 
-    def body(i, carry):
-        def received(a_ref, b_ref):
-            tiles = [jnp.where(even, a_ref[i * 6 + n], b_ref[i * 6 + n]) for n in range(6)]
-            side = [from_spare(tiles[n : n + 3], inner) for n in (0, 3)]
-            return side, tiles[:3], tiles[3:]
-
-        above, below = received(one_ref, two_ref), received(two_ref, one_ref)
-        mine = [[own_ref[(i * 3 + f) * ROWS + j] for j in range(ROWS)] for f in range(3)]
-        u = [None] + above[0] + mine[0] + below[0] + [None]
-        v = above[1] + mine[1] + below[1]
-        h = above[2] + mine[2] + below[2]
-        start = (u, v, h)
-        least = least_ref[i]
-        wave = turn_speed * slope_ref[i]
-        count = ROWS + 2 * HALO
-        keep, zs = [None] * count, [None] * count
-        for j in range(1, count - 1):
-            keep[j] = jnp.where(least <= cut_ref[j : j + 1, :], 1.0, 0.0)
-            zs[j] = wave * band_ref[z, 1, j : j + 1, :]
-
-        def advance(state, margin, scale):
-            su, sv, sh = state
-            vc = [None] * count
-            for j in range(margin - 1, count - margin + 1):
-                vc[j] = sv[j] * band_ref[z, 2, j : j + 1, :]
-            out = ([None] * count, [None] * count, [None] * count)
-            for j in range(margin, count - margin):
-                cor = band_ref[z, 0, j : j + 1, :]
-                tu = cor * sv[j] - zs[j] * pltpu.roll(sh[j], 4, 0)
+    def received(a_ref, b_ref, i):
+        pick = lambda t: jnp.where(even, a_ref[t], b_ref[t])
+        tiles = []
+        for t in range(i * 6, i * 6 + 6):
+            e = 3 * (t - SENT)
+            tiles.append(pick(t) if t < SENT else from_spare([pick(e + c) for c in range(3)], inner))
+        return tiles
+
+    for i in range(PAIRS):
+        above, below = received(one_ref, two_ref, i), received(two_ref, one_ref, i)
+        u, v, h = ([own_ref[(i * 3 + f) * ROWS + j] for j in range(ROWS)] for f in range(3))
+        rows = Rows(z, i, cut_ref, speed, turn_speed, slope_ref, least_ref, band_ref)
+        span = range(-1, ROWS + 1)
+        keep = {j: rows.keep(j) for j in span}
+        zonal = {j: rows.zonal(j) for j in range(ROWS)}
+
+        def advance(state, level, scale):
+            su, sv, sh = state[:3]
+            sv, sh = {j: sv[j] for j in range(ROWS)}, {j: sh[j] for j in range(ROWS)}
+            before, after = above[2 * level : 2 * level + 2], below[2 * level : 2 * level + 2]
+            if level == 0:
+                (sv[-1], sh[-1]), (sv[ROWS], sh[ROWS]) = before, after
+            else:
+                last = ROWS - 1
+                top, end = keep[-1] * state[3], keep[ROWS] * state[3]
+                pv, ph = state[4]
+                sv[-1] = before[0] + top * half_speed * ph[0]
+                sh[-1] = before[1] + top * rows.merid(-1) * (pv[0] * rows.cos(0))
+                sv[ROWS] = after[0] - end * half_speed * ph[last]
+                sh[ROWS] = after[1] - end * rows.merid(ROWS) * (pv[last] * rows.cos(last))
+            vc = {j: sv[j] * rows.cos(j) for j in span}
+            out = [], [], []
+            for j in range(ROWS):
+                cor = rows.cor(j)
+                tu = cor * sv[j] - zonal[j] * swap_parts(sh[j])
                 tv = cor * su[j] + half_speed * (sh[j - 1] - sh[j + 1])
-                th = zs[j] * pltpu.roll(su[j], 4, 0) + (speed * band_ref[z, 3, j : j + 1, :]) * (
-                    vc[j - 1] - vc[j + 1]
-                )
+                th = zonal[j] * swap_parts(su[j]) + rows.merid(j) * (vc[j - 1] - vc[j + 1])
                 if scale is None:
-                    out[0][j], out[1][j], out[2][j] = keep[j] * tu, -keep[j] * tv, -keep[j] * th
+                    values = keep[j] * tu, -keep[j] * tv, -keep[j] * th
                 else:
                     m = keep[j] * scale
-                    out[0][j] = u[j] + m * tu
-                    out[1][j] = v[j] - m * tv
-                    out[2][j] = h[j] - m * th
-            return out
-
-        gain = advance(advance(advance(start, 1, 1.0 / 3.0), 2, 0.5), 3, None)
+                    values = u[j] + m * tu, v[j] - m * tv, h[j] - m * th
+                for into, value in zip(out, values):
+                    into.append(value)
+            return *out, scale, (sv, sh)
+
+        gain = advance((u, v, h), 0, 1.0 / 3.0)
+        gain = advance(gain, 1, 0.5)
+        gain = advance(gain, 2, None)
         for f in range(3):
-            rows = gain[f][HALO : HALO + ROWS]
-            north, south = swap_lane(rows[0], rows[1], lane), swap_lane(rows[2], rows[3], lane)
+            r = gain[f]
+            north, south = swap_lane(r[0], r[1], lane), swap_lane(r[2], r[3], lane)
             for side in range(2):
                 re, im = swap_sub(north[side], south[side], sub)
                 at = (f * 2 * PAIRS + side) * 16 + i * 32
                 split_store(x_ref, pl.ds(at, 16), re, im)
-        return carry
-
-    for i in range(PAIRS):
-        body(i, 0)
-    y_ref[...] = jnp.dot(x_ref[...], dft_ref[...], preferred_element_type=jnp.float32)
     for f in (2, 0, 1):
+        field_dot(y_ref, x_ref, dft_ref, f, 2 * PAIRS)
         spec = []
         for k in range(NK):
             at = (f * 2 * PAIRS + k) * 16
@@ -422,10 +495,10 @@
         forward_kernel,
         out_shape=(
             shaped(PAIRS * 3 * ROWS, 8, 128),
-            shaped(PAIRS * 6, 8, 128),
-            shaped(PAIRS * 6, 8, 128),
+            shaped(SENT, 8, 128),
+            shaped(SENT, 8, 128),
         ),
-        in_specs=vmem(3),
+        in_specs=vmem(8),
         out_specs=tuple(vmem(3)),
         scratch_shapes=[
             pltpu.VMEM((3 * NK * 16, 768), jnp.bfloat16),
@@ -433,7 +506,7 @@
         ],
         name="forward",
         compiler_params=PARAMS,
-    )(circles, dft, twid)
+    )(circles, dft, twid, cut_rows, speeds, slope, least, per_band)
     stop = bands - 1
     south = [[(2 * i + c, 2 * i + 2 + c) for i in range(stop)] for c in range(2)]
     north = [[(b, a) for a, b in pairs] for pairs in south]

time: 50.2 us -> 49.6 us (0.988)
  waiting for transfers between devices: 3.97 us -> 2.83 us
    ppermute x1, waiting for transfers between devices: 2.59 us -> 2.02 us  [shards(): two = lax.ppermute(two, ('lat', 'lon_2'), north[0] + south[1])]
    ppermute x1, waiting for transfers between devices: 1.38 us -> 0.81 us  [shards(): one = lax.ppermute(one, ('lat', 'lon_2'), south[0] + north[1])]
    all_to_all x1, blocking collectives: 16.6 us -> 17.1 us  [shards(): waves = lax.all_to_all(waves, LON, 0, 0, tiled=True)]
where the time goes in v2:
time: 49.6 us; the launch traced here: 49.3 us
  blocking collectives  34.3 us (69%)
  starting transfers between devices  6.68 us (13%)
  Pallas kernels  4.64 us (9%)
  waiting for transfers between devices  2.83 us (6%)
  between operations  0.77 us (2%)
    all_to_all x1, blocking collectives, shards(): circles = lax.all_to_all(packed, LON, 0, 0, tiled=True)  17.2 us
    all_to_all x1, blocking collectives, shards(): waves = lax.all_to_all(waves, LON, 0, 0, tiled=True)  17.1 us
    ppermute x1, starting transfers between devices, shards(): two = lax.ppermute(two, ('lat', 'lon_2'), north[0] + south[1])  4.76 us
    ppermute x1, waiting for transfers between devices, shards(): two = lax.ppermute(two, ('lat', 'lon_2'), north[0] + south[1])  2.02 us
    ppermute x1, starting transfers between devices, shards(): one = lax.ppermute(one, ('lat', 'lon_2'), south[0] + north[1])  1.92 us
    pallas_call x1, Pallas kernels, shards(): pl.pallas_call(pack_kernel, out_shape=(shaped(NB, SLOTS, LV, 128), jax.Sh...  1.49 us
    pallas_call x1, Pallas kernels, shards(): pl.pallas_call(unpack_kernel, out_shape=tuple((shaped(NR, ROWS, levels) f...  1.24 us
    pallas_call x1, Pallas kernels, shards(): pl.pallas_call(step_kernel, out_shape=shaped(NB, SLOTS, LV, 128), in_spec...  1.07 us
  transfers between devices with their start and end apart: 2, of which 2 were waited for; matrix products, arithmetic and copies ran while one was open for 0% of the time, Pallas kernels for 0%

profile of v2, /device:TPU:97, one launch (start us, length us, event | category | flops | bytes accessed | tf_op | source)
XLA Modules:
  0.0 49.3 jit_solution(10104297903892585750)
XLA Ops:
  0.6 0.0 copy-start.6
  0.6 0.0 copy-start.7
  0.7 1.5 %pack.1 = (f32[32,5,4,128]{3,2,1,0:T(4,128)S(1)}, s32[16,128]{1,0:T(8,128)S(1)}, f32[8,128]{1,0:T(8,128)S(1)}) custom-call(f32[45,4,128]{2,1,0:T(4,128)} %u_ref.1, f32[45,4,128]{2,1,0:T(4,128)} %v_ref.1, f32[45,4,128]{2,1,0:T(4,128)} %h_ref.1, s32[32]{0:T(128)} %cut_hbm.1, f32[128]{0:T(128)} %speed_hbm.1), custom_call_target="tpu_custom_call" | custom-call | tf_op jit(solution)/shard_map/pack/pallas_call | solution.py:474
  2.2 0.0 copy-start
  2.2 0.0 copy-start.1
  2.2 0.0 copy-start.5
  2.2 17.2 %all_to_all.10.z_ref = f32[32,5,4,128]{3,2,1,0:T(4,128)S(1)} all-to-all(f32[32,5,4,128]{3,2,1,0:T(4,128)S(1)} %get-tuple-element.9), channel_id=1, replica_groups=mesh['lat'=8,'lon_0'=4,'lon_1'=4,'lon_2'=2] {'lon_0','lon_1','lon_2'}, dimensions={0} | all-to-all | bytes 655360 | tf_op jit(solution)/shard_map/all_to_all | solution.py:493
  19.4 0.0 copy-done.6
  19.4 0.0 copy-done.7
  19.4 0.0 copy-done
  19.4 0.0 copy-done.1
  19.4 0.0 copy-done.5
  19.4 0.0 copy-start.8
  19.4 0.8 %forward.1 = (f32[108,8,128]{2,1,0:T(8,128)S(1)}, f32[41,8,128]{2,1,0:T(8,128)S(1)}, f32[41,8,128]{2,1,0:T(8,128)S(1)}) custom-call(f32[32,5,4,128]{3,2,1,0:T(4,128)S(1)} %all_to_all.10.z_ref, bf16[768,256]{1,0:T(8,128)(2,1)S(1)} %copy-done, f32[17,2,128]{2,1,0:T(2,128)S(1)} %copy-done.7, s32[16,128]{1,0:T(8,128)S(1)} %get-tuple-element.10.cut_ref, ...), custom_call_target="tpu_custom_call" | custom-call | tf_op jit(solution)/shard_map/forward/pallas_call | solution.py:494
  20.3 1.9 %collective-permute-start = (f32[41,8,128]{2,1,0:T(8,128)S(1)}, f32[41,8,128]{2,1,0:T(8,128)S(1)}, u32[]{:S(2)}, u32[]{:S(2)}) collective-permute-start(f32[41,8,128]{2,1,0:T(8,128)S(1)} %get-tuple-element.13), channel_id=1, source_target_pairs={{0,32},{32,64},{64,96},{96,128},{128,160},{160,192},{192,224},{33,... | collective-permute-start | bytes 503816 | tf_op jit(solution)/shard_map/ppermute | solution.py:513
  22.2 4.8 %collective-permute-start.1 = (f32[41,8,128]{2,1,0:T(8,128)S(1)}, f32[41,8,128]{2,1,0:T(8,128)S(1)}, u32[]{:S(2)}, u32[]{:S(2)}) collective-permute-start(f32[41,8,128]{2,1,0:T(8,128)S(1)} %get-tuple-element.14), channel_id=1, source_target_pairs={{32,0},{64,32},{96,64},{128,96},{160,128},{192,160},{224,192},{1,3... | collective-permute-start | bytes 503816 | tf_op jit(solution)/shard_map/ppermute | solution.py:514
  27.0 0.8 %collective-permute-done.one_ref = f32[41,8,128]{2,1,0:T(8,128)S(1)} collective-permute-done((f32[41,8,128]{2,1,0:T(8,128)S(1)}, f32[41,8,128]{2,1,0:T(8,128)S(1)}, u32[]{:S(2)}, u32[]{:S(2)}) %collective-permute-start) | collective-permute-done | bytes 167968 | tf_op jit(solution)/shard_map/ppermute | solution.py:513
  27.8 2.0 %collective-permute-done.1.two_ref = f32[41,8,128]{2,1,0:T(8,128)S(1)} collective-permute-done((f32[41,8,128]{2,1,0:T(8,128)S(1)}, f32[41,8,128]{2,1,0:T(8,128)S(1)}, u32[]{:S(2)}, u32[]{:S(2)}) %collective-permute-start.1) | collective-permute-done | bytes 167968 | tf_op jit(solution)/shard_map/ppermute | solution.py:514
  29.8 0.0 copy-done.8
  29.8 1.1 %sections.1 = f32[32,5,4,128]{3,2,1,0:T(4,128)S(1)} custom-call(f32[108,8,128]{2,1,0:T(8,128)S(1)} %get-tuple-element.12.own_ref, f32[41,8,128]{2,1,0:T(8,128)S(1)} %collective-permute-done.one_ref, f32[41,8,128]{2,1,0:T(8,128)S(1)} %collective-permute-done.1.two_ref, s32[16,128]{1,0:T(8,128)S(1)} %get-tuple-element.10.cut_ref, ...), custom_call_target="tpu_custom_call" | custom-call | tf_op jit(solution)/shard_map/sections/pallas_call | solution.py:515
  30.9 0.0 copy-start.2
  30.9 0.0 copy-start.3
  30.9 0.0 copy-start.4
  30.9 17.1 %all_to_all.11.w_ref = f32[32,5,4,128]{3,2,1,0:T(4,128)S(1)} all-to-all(f32[32,5,4,128]{3,2,1,0:T(4,128)S(1)} %sections.1), channel_id=1, replica_groups=mesh['lat'=8,'lon_0'=4,'lon_1'=4,'lon_2'=2] {'lon_0','lon_1','lon_2'}, dimensions={0} | all-to-all | bytes 655360 | tf_op jit(solution)/shard_map/all_to_all | solution.py:528
  48.1 0.0 copy-done.2
  48.1 0.0 copy-done.3
  48.1 0.0 copy-done.4
  48.1 1.2 %unpack.1 = (f32[45,4,128]{2,1,0:T(4,128)}, f32[45,4,128]{2,1,0:T(4,128)}, f32[45,4,128]{2,1,0:T(4,128)}) custom-call(f32[32,5,4,128]{3,2,1,0:T(4,128)S(1)} %all_to_all.11.w_ref, f32[45,4,128]{2,1,0:T(4,128)S(1)} %copy-done.2, f32[45,4,128]{2,1,0:T(4,128)S(1)} %copy-done.3, f32[45,4,128]{2,1,0:T(4,128)S(1)} %copy-done.4), custom_call_target="tpu_custom_call" | custom-call | tf_op jit(solution)/shard_map/unpack/pallas_call | solution.py:529
Async XLA Ops:
  0.6 18.8 %copy-start.6 = (f32[9,1,128]{2,1,0:T(1,128)S(1)}, f32[9,1,128]{2,1,0:T(1,128)}, u32[]{:S(2)}) copy-start(f32[9,1,128]{2,1,0:T(1,128)} %constant.15.clone.slope_ref) | copy-start | bytes 13828
  0.6 18.8 %copy-start.7 = (f32[17,2,128]{2,1,0:T(2,128)S(1)}, f32[17,2,128]{2,1,0:T(2,128)}, u32[]{:S(2)}) copy-start(f32[17,2,128]{2,1,0:T(2,128)} %constant.13.clone.tw_ref) | copy-start | bytes 52228
  2.2 17.2 %copy-start = (bf16[768,256]{1,0:T(8,128)(2,1)S(1)}, bf16[768,256]{1,0:T(8,128)(2,1)}, u32[]{:S(2)}) copy-start(bf16[768,256]{1,0:T(8,128)(2,1)} %constant.12.clone.dft_ref) | copy-start | bytes 1179652
  2.2 17.2 %copy-start.1 = (f32[8,4,16,128]{3,2,1,0:T(8,128)S(1)}, f32[8,4,16,128]{3,2,1,0:T(8,128)}, u32[]{:S(2)}) copy-start(f32[8,4,16,128]{3,2,1,0:T(8,128)} %constant.17.clone.band_ref) | copy-start | bytes 786436
  2.2 17.2 %copy-start.5 = (s32[9,1,128]{2,1,0:T(1,128)S(1)}, s32[9,1,128]{2,1,0:T(1,128)}, u32[]{:S(2)}) copy-start(s32[9,1,128]{2,1,0:T(1,128)} %constant.16.clone.least_ref) | copy-start | bytes 13828
  19.4 10.4 %copy-start.8 = (f32[17,2,128]{2,1,0:T(2,128)S(1)}, f32[17,2,128]{2,1,0:T(2,128)}, u32[]{:S(2)}) copy-start(f32[17,2,128]{2,1,0:T(2,128)} %constant.14.clone.tw_ref) | copy-start | bytes 52228
  20.3 7.5 %collective-permute-start = (f32[41,8,128]{2,1,0:T(8,128)S(1)}, f32[41,8,128]{2,1,0:T(8,128)S(1)}, u32[]{:S(2)}, u32[]{:S(2)}) collective-permute-start(f32[41,8,128]{2,1,0:T(8,128)S(1)} %get-tuple-element.13), channel_id=1, source_target_pairs={{0,32},{32,64},{64,96},{96,128},{128,160},{160,192},{192,224},{33,... | collective-permute-start | bytes 503816 | tf_op jit(solution)/shard_map/ppermute | solution.py:513
  22.2 7.6 %collective-permute-start.1 = (f32[41,8,128]{2,1,0:T(8,128)S(1)}, f32[41,8,128]{2,1,0:T(8,128)S(1)}, u32[]{:S(2)}, u32[]{:S(2)}) collective-permute-start(f32[41,8,128]{2,1,0:T(8,128)S(1)} %get-tuple-element.14), channel_id=1, source_target_pairs={{32,0},{64,32},{96,64},{128,96},{160,128},{192,160},{224,192},{1,3... | collective-permute-start | bytes 503816 | tf_op jit(solution)/shard_map/ppermute | solution.py:514
  30.9 17.2 %copy-start.2 = (f32[45,4,128]{2,1,0:T(4,128)S(1)}, f32[45,4,128]{2,1,0:T(4,128)}, u32[]{:S(2)}) copy-start(f32[45,4,128]{2,1,0:T(4,128)} %u_ref.1) | copy-start | bytes 276484
  30.9 17.2 %copy-start.3 = (f32[45,4,128]{2,1,0:T(4,128)S(1)}, f32[45,4,128]{2,1,0:T(4,128)}, u32[]{:S(2)}) copy-start(f32[45,4,128]{2,1,0:T(4,128)} %v_ref.1) | copy-start | bytes 276484
  30.9 17.2 %copy-start.4 = (f32[45,4,128]{2,1,0:T(4,128)S(1)}, f32[45,4,128]{2,1,0:T(4,128)}, u32[]{:S(2)}) copy-start(f32[45,4,128]{2,1,0:T(4,128)} %h_ref.1) | copy-start | bytes 276484

commit v3 on v2

--- a/solution.py
+++ b/solution.py
@@ -404,15 +404,15 @@
         for f in range(3):
             r = gain[f]
             north, south = swap_lane(r[0], r[1], lane), swap_lane(r[2], r[3], lane)
-            for side in range(2):
+            for side in range(min(2, NK - 2 * i)):
                 re, im = swap_sub(north[side], south[side], sub)
-                at = (f * 2 * PAIRS + side) * 16 + i * 32
+                at = (f * NK + 2 * i + side) * 16
                 split_store(x_ref, pl.ds(at, 16), re, im)
     for f in (2, 0, 1):
-        field_dot(y_ref, x_ref, dft_ref, f, 2 * PAIRS)
+        field_dot(y_ref, x_ref, dft_ref, f, NK)
         spec = []
         for k in range(NK):
-            at = (f * 2 * PAIRS + k) * 16
+            at = (f * NK + k) * 16
             a = y_ref[at : at + 8, :128] - y_ref[at + 8 : at + 16, 128:]
             b = y_ref[at + 8 : at + 16, :128] + y_ref[at : at + 8, 128:]
             c, s = tw_ref[k, 0:1, :], tw_ref[k, 1:2, :]
@@ -518,8 +518,8 @@
         in_specs=vmem(10),
         out_specs=vmem(1)[0],
         scratch_shapes=[
-            pltpu.VMEM((3 * 2 * PAIRS * 16, 768), jnp.bfloat16),
-            pltpu.VMEM((3 * 2 * PAIRS * 16, 256), jnp.float32),
+            pltpu.VMEM((3 * NK * 16, 768), jnp.bfloat16),
+            pltpu.VMEM((3 * NK * 16, 256), jnp.float32),
             pltpu.VMEM((NB, 2 * LV, 128), jnp.float32),
         ],
         name="sections",

time: 49.6 us -> 49.6 us (level)
  no operation moved by 1% of the time
where the time goes in v3:
time: 49.6 us; the launch traced here: 49.3 us
  blocking collectives  34.3 us (69%)
  starting transfers between devices  6.68 us (13%)
  Pallas kernels  4.63 us (9%)
  waiting for transfers between devices  2.83 us (6%)
  between operations  0.77 us (2%)
    all_to_all x1, blocking collectives, shards(): circles = lax.all_to_all(packed, LON, 0, 0, tiled=True)  17.2 us
    all_to_all x1, blocking collectives, shards(): waves = lax.all_to_all(waves, LON, 0, 0, tiled=True)  17.1 us
    ppermute x1, starting transfers between devices, shards(): two = lax.ppermute(two, ('lat', 'lon_2'), north[0] + south[1])  4.76 us
    ppermute x1, waiting for transfers between devices, shards(): two = lax.ppermute(two, ('lat', 'lon_2'), north[0] + south[1])  2.02 us
    ppermute x1, starting transfers between devices, shards(): one = lax.ppermute(one, ('lat', 'lon_2'), south[0] + north[1])  1.92 us
    pallas_call x1, Pallas kernels, shards(): pl.pallas_call(pack_kernel, out_shape=(shaped(NB, SLOTS, LV, 128), jax.Sh...  1.49 us
    pallas_call x1, Pallas kernels, shards(): pl.pallas_call(unpack_kernel, out_shape=tuple((shaped(NR, ROWS, levels) f...  1.24 us
    pallas_call x1, Pallas kernels, shards(): pl.pallas_call(step_kernel, out_shape=shaped(NB, SLOTS, LV, 128), in_spec...  1.05 us
  transfers between devices with their start and end apart: 2, of which 2 were waited for; matrix products, arithmetic and copies ran while one was open for 0% of the time, Pallas kernels for 0%

profile of v3, /device:TPU:97, one launch (start us, length us, event | category | flops | bytes accessed | tf_op | source)
XLA Modules:
  0.0 49.3 jit_solution(16965575513966583802)
XLA Ops:
  0.6 0.0 copy-start.6
  0.6 0.0 copy-start.7
  0.7 1.5 %pack.1 = (f32[32,5,4,128]{3,2,1,0:T(4,128)S(1)}, s32[16,128]{1,0:T(8,128)S(1)}, f32[8,128]{1,0:T(8,128)S(1)}) custom-call(f32[45,4,128]{2,1,0:T(4,128)} %u_ref.1, f32[45,4,128]{2,1,0:T(4,128)} %v_ref.1, f32[45,4,128]{2,1,0:T(4,128)} %h_ref.1, s32[32]{0:T(128)} %cut_hbm.1, f32[128]{0:T(128)} %speed_hbm.1), custom_call_target="tpu_custom_call" | custom-call | tf_op jit(solution)/shard_map/pack/pallas_call | solution.py:474
  2.2 0.0 copy-start
  2.2 0.0 copy-start.1
  2.2 0.0 copy-start.5
  2.2 17.2 %all_to_all.10.z_ref = f32[32,5,4,128]{3,2,1,0:T(4,128)S(1)} all-to-all(f32[32,5,4,128]{3,2,1,0:T(4,128)S(1)} %get-tuple-element.9), channel_id=1, replica_groups=mesh['lat'=8,'lon_0'=4,'lon_1'=4,'lon_2'=2] {'lon_0','lon_1','lon_2'}, dimensions={0} | all-to-all | bytes 655360 | tf_op jit(solution)/shard_map/all_to_all | solution.py:493
  19.4 0.0 copy-done.6
  19.4 0.0 copy-done.7
  19.4 0.0 copy-done
  19.4 0.0 copy-done.1
  19.4 0.0 copy-done.5
  19.4 0.0 copy-start.8
  19.4 0.8 %forward.1 = (f32[108,8,128]{2,1,0:T(8,128)S(1)}, f32[41,8,128]{2,1,0:T(8,128)S(1)}, f32[41,8,128]{2,1,0:T(8,128)S(1)}) custom-call(f32[32,5,4,128]{3,2,1,0:T(4,128)S(1)} %all_to_all.10.z_ref, bf16[768,256]{1,0:T(8,128)(2,1)S(1)} %copy-done, f32[17,2,128]{2,1,0:T(2,128)S(1)} %copy-done.7, s32[16,128]{1,0:T(8,128)S(1)} %get-tuple-element.10.cut_ref, ...), custom_call_target="tpu_custom_call" | custom-call | tf_op jit(solution)/shard_map/forward/pallas_call | solution.py:494
  20.3 1.9 %collective-permute-start = (f32[41,8,128]{2,1,0:T(8,128)S(1)}, f32[41,8,128]{2,1,0:T(8,128)S(1)}, u32[]{:S(2)}, u32[]{:S(2)}) collective-permute-start(f32[41,8,128]{2,1,0:T(8,128)S(1)} %get-tuple-element.13), channel_id=1, source_target_pairs={{0,32},{32,64},{64,96},{96,128},{128,160},{160,192},{192,224},{33,... | collective-permute-start | bytes 503816 | tf_op jit(solution)/shard_map/ppermute | solution.py:513
  22.2 4.8 %collective-permute-start.1 = (f32[41,8,128]{2,1,0:T(8,128)S(1)}, f32[41,8,128]{2,1,0:T(8,128)S(1)}, u32[]{:S(2)}, u32[]{:S(2)}) collective-permute-start(f32[41,8,128]{2,1,0:T(8,128)S(1)} %get-tuple-element.14), channel_id=1, source_target_pairs={{32,0},{64,32},{96,64},{128,96},{160,128},{192,160},{224,192},{1,3... | collective-permute-start | bytes 503816 | tf_op jit(solution)/shard_map/ppermute | solution.py:514
  27.0 0.8 %collective-permute-done.one_ref = f32[41,8,128]{2,1,0:T(8,128)S(1)} collective-permute-done((f32[41,8,128]{2,1,0:T(8,128)S(1)}, f32[41,8,128]{2,1,0:T(8,128)S(1)}, u32[]{:S(2)}, u32[]{:S(2)}) %collective-permute-start) | collective-permute-done | bytes 167968 | tf_op jit(solution)/shard_map/ppermute | solution.py:513
  27.8 2.0 %collective-permute-done.1.two_ref = f32[41,8,128]{2,1,0:T(8,128)S(1)} collective-permute-done((f32[41,8,128]{2,1,0:T(8,128)S(1)}, f32[41,8,128]{2,1,0:T(8,128)S(1)}, u32[]{:S(2)}, u32[]{:S(2)}) %collective-permute-start.1) | collective-permute-done | bytes 167968 | tf_op jit(solution)/shard_map/ppermute | solution.py:514
  29.8 0.0 copy-done.8
  29.8 1.1 %sections.1 = f32[32,5,4,128]{3,2,1,0:T(4,128)S(1)} custom-call(f32[108,8,128]{2,1,0:T(8,128)S(1)} %get-tuple-element.12.own_ref, f32[41,8,128]{2,1,0:T(8,128)S(1)} %collective-permute-done.one_ref, f32[41,8,128]{2,1,0:T(8,128)S(1)} %collective-permute-done.1.two_ref, s32[16,128]{1,0:T(8,128)S(1)} %get-tuple-element.10.cut_ref, ...), custom_call_target="tpu_custom_call" | custom-call | tf_op jit(solution)/shard_map/sections/pallas_call | solution.py:515
  30.9 0.0 copy-start.2
  30.9 0.0 copy-start.3
  30.9 0.0 copy-start.4
  30.9 17.1 %all_to_all.11.w_ref = f32[32,5,4,128]{3,2,1,0:T(4,128)S(1)} all-to-all(f32[32,5,4,128]{3,2,1,0:T(4,128)S(1)} %sections.1), channel_id=1, replica_groups=mesh['lat'=8,'lon_0'=4,'lon_1'=4,'lon_2'=2] {'lon_0','lon_1','lon_2'}, dimensions={0} | all-to-all | bytes 655360 | tf_op jit(solution)/shard_map/all_to_all | solution.py:528
  48.1 0.0 copy-done.2
  48.1 0.0 copy-done.3
  48.1 0.0 copy-done.4
  48.1 1.2 %unpack.1 = (f32[45,4,128]{2,1,0:T(4,128)}, f32[45,4,128]{2,1,0:T(4,128)}, f32[45,4,128]{2,1,0:T(4,128)}) custom-call(f32[32,5,4,128]{3,2,1,0:T(4,128)S(1)} %all_to_all.11.w_ref, f32[45,4,128]{2,1,0:T(4,128)S(1)} %copy-done.2, f32[45,4,128]{2,1,0:T(4,128)S(1)} %copy-done.3, f32[45,4,128]{2,1,0:T(4,128)S(1)} %copy-done.4), custom_call_target="tpu_custom_call" | custom-call | tf_op jit(solution)/shard_map/unpack/pallas_call | solution.py:529
Async XLA Ops:
  0.6 18.8 %copy-start.6 = (f32[9,1,128]{2,1,0:T(1,128)S(1)}, f32[9,1,128]{2,1,0:T(1,128)}, u32[]{:S(2)}) copy-start(f32[9,1,128]{2,1,0:T(1,128)} %constant.15.clone.slope_ref) | copy-start | bytes 13828
  0.6 18.8 %copy-start.7 = (f32[17,2,128]{2,1,0:T(2,128)S(1)}, f32[17,2,128]{2,1,0:T(2,128)}, u32[]{:S(2)}) copy-start(f32[17,2,128]{2,1,0:T(2,128)} %constant.13.clone.tw_ref) | copy-start | bytes 52228
  2.2 17.2 %copy-start = (bf16[768,256]{1,0:T(8,128)(2,1)S(1)}, bf16[768,256]{1,0:T(8,128)(2,1)}, u32[]{:S(2)}) copy-start(bf16[768,256]{1,0:T(8,128)(2,1)} %constant.12.clone.dft_ref) | copy-start | bytes 1179652
  2.2 17.2 %copy-start.1 = (f32[8,4,16,128]{3,2,1,0:T(8,128)S(1)}, f32[8,4,16,128]{3,2,1,0:T(8,128)}, u32[]{:S(2)}) copy-start(f32[8,4,16,128]{3,2,1,0:T(8,128)} %constant.17.clone.band_ref) | copy-start | bytes 786436
  2.2 17.2 %copy-start.5 = (s32[9,1,128]{2,1,0:T(1,128)S(1)}, s32[9,1,128]{2,1,0:T(1,128)}, u32[]{:S(2)}) copy-start(s32[9,1,128]{2,1,0:T(1,128)} %constant.16.clone.least_ref) | copy-start | bytes 13828
  19.4 10.4 %copy-start.8 = (f32[17,2,128]{2,1,0:T(2,128)S(1)}, f32[17,2,128]{2,1,0:T(2,128)}, u32[]{:S(2)}) copy-start(f32[17,2,128]{2,1,0:T(2,128)} %constant.14.clone.tw_ref) | copy-start | bytes 52228
  20.3 7.5 %collective-permute-start = (f32[41,8,128]{2,1,0:T(8,128)S(1)}, f32[41,8,128]{2,1,0:T(8,128)S(1)}, u32[]{:S(2)}, u32[]{:S(2)}) collective-permute-start(f32[41,8,128]{2,1,0:T(8,128)S(1)} %get-tuple-element.13), channel_id=1, source_target_pairs={{0,32},{32,64},{64,96},{96,128},{128,160},{160,192},{192,224},{33,... | collective-permute-start | bytes 503816 | tf_op jit(solution)/shard_map/ppermute | solution.py:513
  22.2 7.6 %collective-permute-start.1 = (f32[41,8,128]{2,1,0:T(8,128)S(1)}, f32[41,8,128]{2,1,0:T(8,128)S(1)}, u32[]{:S(2)}, u32[]{:S(2)}) collective-permute-start(f32[41,8,128]{2,1,0:T(8,128)S(1)} %get-tuple-element.14), channel_id=1, source_target_pairs={{32,0},{64,32},{96,64},{128,96},{160,128},{192,160},{224,192},{1,3... | collective-permute-start | bytes 503816 | tf_op jit(solution)/shard_map/ppermute | solution.py:514
  30.9 17.2 %copy-start.2 = (f32[45,4,128]{2,1,0:T(4,128)S(1)}, f32[45,4,128]{2,1,0:T(4,128)}, u32[]{:S(2)}) copy-start(f32[45,4,128]{2,1,0:T(4,128)} %u_ref.1) | copy-start | bytes 276484
  30.9 17.2 %copy-start.3 = (f32[45,4,128]{2,1,0:T(4,128)S(1)}, f32[45,4,128]{2,1,0:T(4,128)}, u32[]{:S(2)}) copy-start(f32[45,4,128]{2,1,0:T(4,128)} %v_ref.1) | copy-start | bytes 276484
  30.9 17.2 %copy-start.4 = (f32[45,4,128]{2,1,0:T(4,128)S(1)}, f32[45,4,128]{2,1,0:T(4,128)}, u32[]{:S(2)}) copy-start(f32[45,4,128]{2,1,0:T(4,128)} %h_ref.1) | copy-start | bytes 276484

commit v4 on v3

--- a/solution.py
+++ b/solution.py
@@ -150,7 +150,8 @@
     ]
     for copy in fields + small:
         copy.start()
-    tmp[...] = jnp.zeros_like(tmp)
+    for side in (0, 64):
+        tmp[:, :, side + 40 : side + 64, :] = jnp.zeros((3, 2, 24, 128), jnp.float32)
     inner = lax.broadcasted_iota(jnp.int32, (128, 128), 1) % 64
     extra = None
     for f, copy in zip((2, 0, 1), fields):

time: 49.6 us -> 49.6 us (level)
  no operation moved by 1% of the time
where the time goes in v4:
time: 49.6 us; the launch traced here: 49.3 us
  blocking collectives  34.3 us (69%)
  starting transfers between devices  6.68 us (13%)
  Pallas kernels  4.63 us (9%)
  waiting for transfers between devices  2.83 us (6%)
  between operations  0.77 us (2%)
    all_to_all x1, blocking collectives, shards(): circles = lax.all_to_all(packed, LON, 0, 0, tiled=True)  17.2 us
    all_to_all x1, blocking collectives, shards(): waves = lax.all_to_all(waves, LON, 0, 0, tiled=True)  17.1 us
    ppermute x1, starting transfers between devices, shards(): two = lax.ppermute(two, ('lat', 'lon_2'), north[0] + south[1])  4.76 us
    ppermute x1, waiting for transfers between devices, shards(): two = lax.ppermute(two, ('lat', 'lon_2'), north[0] + south[1])  2.02 us
    ppermute x1, starting transfers between devices, shards(): one = lax.ppermute(one, ('lat', 'lon_2'), south[0] + north[1])  1.92 us
    pallas_call x1, Pallas kernels, shards(): pl.pallas_call(pack_kernel, out_shape=(shaped(NB, SLOTS, LV, 128), jax.Sh...  1.49 us
    pallas_call x1, Pallas kernels, shards(): pl.pallas_call(unpack_kernel, out_shape=tuple((shaped(NR, ROWS, levels) f...  1.24 us
    pallas_call x1, Pallas kernels, shards(): pl.pallas_call(step_kernel, out_shape=shaped(NB, SLOTS, LV, 128), in_spec...  1.05 us
  transfers between devices with their start and end apart: 2, of which 2 were waited for; matrix products, arithmetic and copies ran while one was open for 0% of the time, Pallas kernels for 0%

profile of v4, /device:TPU:97, one launch (start us, length us, event | category | flops | bytes accessed | tf_op | source)
XLA Modules:
  0.0 49.3 jit_solution(11251179601617904694)
XLA Ops:
  0.6 0.0 copy-start.6
  0.6 0.0 copy-start.7
  0.7 1.5 %pack.1 = (f32[32,5,4,128]{3,2,1,0:T(4,128)S(1)}, s32[16,128]{1,0:T(8,128)S(1)}, f32[8,128]{1,0:T(8,128)S(1)}) custom-call(f32[45,4,128]{2,1,0:T(4,128)} %u_ref.1, f32[45,4,128]{2,1,0:T(4,128)} %v_ref.1, f32[45,4,128]{2,1,0:T(4,128)} %h_ref.1, s32[32]{0:T(128)} %cut_hbm.1, f32[128]{0:T(128)} %speed_hbm.1), custom_call_target="tpu_custom_call" | custom-call | tf_op jit(solution)/shard_map/pack/pallas_call | solution.py:475
  2.2 0.0 copy-start
  2.2 0.0 copy-start.1
  2.2 0.0 copy-start.5
  2.2 17.2 %all_to_all.10.z_ref = f32[32,5,4,128]{3,2,1,0:T(4,128)S(1)} all-to-all(f32[32,5,4,128]{3,2,1,0:T(4,128)S(1)} %get-tuple-element.9), channel_id=1, replica_groups=mesh['lat'=8,'lon_0'=4,'lon_1'=4,'lon_2'=2] {'lon_0','lon_1','lon_2'}, dimensions={0} | all-to-all | bytes 655360 | tf_op jit(solution)/shard_map/all_to_all | solution.py:494
  19.4 0.0 copy-done.6
  19.4 0.0 copy-done.7
  19.4 0.0 copy-done
  19.4 0.0 copy-done.1
  19.4 0.0 copy-done.5
  19.4 0.0 copy-start.8
  19.4 0.8 %forward.1 = (f32[108,8,128]{2,1,0:T(8,128)S(1)}, f32[41,8,128]{2,1,0:T(8,128)S(1)}, f32[41,8,128]{2,1,0:T(8,128)S(1)}) custom-call(f32[32,5,4,128]{3,2,1,0:T(4,128)S(1)} %all_to_all.10.z_ref, bf16[768,256]{1,0:T(8,128)(2,1)S(1)} %copy-done, f32[17,2,128]{2,1,0:T(2,128)S(1)} %copy-done.7, s32[16,128]{1,0:T(8,128)S(1)} %get-tuple-element.10.cut_ref, ...), custom_call_target="tpu_custom_call" | custom-call | tf_op jit(solution)/shard_map/forward/pallas_call | solution.py:495
  20.3 1.9 %collective-permute-start = (f32[41,8,128]{2,1,0:T(8,128)S(1)}, f32[41,8,128]{2,1,0:T(8,128)S(1)}, u32[]{:S(2)}, u32[]{:S(2)}) collective-permute-start(f32[41,8,128]{2,1,0:T(8,128)S(1)} %get-tuple-element.13), channel_id=1, source_target_pairs={{0,32},{32,64},{64,96},{96,128},{128,160},{160,192},{192,224},{33,... | collective-permute-start | bytes 503816 | tf_op jit(solution)/shard_map/ppermute | solution.py:514
  22.2 4.8 %collective-permute-start.1 = (f32[41,8,128]{2,1,0:T(8,128)S(1)}, f32[41,8,128]{2,1,0:T(8,128)S(1)}, u32[]{:S(2)}, u32[]{:S(2)}) collective-permute-start(f32[41,8,128]{2,1,0:T(8,128)S(1)} %get-tuple-element.14), channel_id=1, source_target_pairs={{32,0},{64,32},{96,64},{128,96},{160,128},{192,160},{224,192},{1,3... | collective-permute-start | bytes 503816 | tf_op jit(solution)/shard_map/ppermute | solution.py:515
  27.0 0.8 %collective-permute-done.one_ref = f32[41,8,128]{2,1,0:T(8,128)S(1)} collective-permute-done((f32[41,8,128]{2,1,0:T(8,128)S(1)}, f32[41,8,128]{2,1,0:T(8,128)S(1)}, u32[]{:S(2)}, u32[]{:S(2)}) %collective-permute-start) | collective-permute-done | bytes 167968 | tf_op jit(solution)/shard_map/ppermute | solution.py:514
  27.8 2.0 %collective-permute-done.1.two_ref = f32[41,8,128]{2,1,0:T(8,128)S(1)} collective-permute-done((f32[41,8,128]{2,1,0:T(8,128)S(1)}, f32[41,8,128]{2,1,0:T(8,128)S(1)}, u32[]{:S(2)}, u32[]{:S(2)}) %collective-permute-start.1) | collective-permute-done | bytes 167968 | tf_op jit(solution)/shard_map/ppermute | solution.py:515
  29.8 0.0 copy-done.8
  29.8 1.1 %sections.1 = f32[32,5,4,128]{3,2,1,0:T(4,128)S(1)} custom-call(f32[108,8,128]{2,1,0:T(8,128)S(1)} %get-tuple-element.12.own_ref, f32[41,8,128]{2,1,0:T(8,128)S(1)} %collective-permute-done.one_ref, f32[41,8,128]{2,1,0:T(8,128)S(1)} %collective-permute-done.1.two_ref, s32[16,128]{1,0:T(8,128)S(1)} %get-tuple-element.10.cut_ref, ...), custom_call_target="tpu_custom_call" | custom-call | tf_op jit(solution)/shard_map/sections/pallas_call | solution.py:516
  30.9 0.0 copy-start.2
  30.9 0.0 copy-start.3
  30.9 0.0 copy-start.4
  30.9 17.1 %all_to_all.11.w_ref = f32[32,5,4,128]{3,2,1,0:T(4,128)S(1)} all-to-all(f32[32,5,4,128]{3,2,1,0:T(4,128)S(1)} %sections.1), channel_id=1, replica_groups=mesh['lat'=8,'lon_0'=4,'lon_1'=4,'lon_2'=2] {'lon_0','lon_1','lon_2'}, dimensions={0} | all-to-all | bytes 655360 | tf_op jit(solution)/shard_map/all_to_all | solution.py:529
  48.1 0.0 copy-done.2
  48.1 0.0 copy-done.3
  48.1 0.0 copy-done.4
  48.1 1.2 %unpack.1 = (f32[45,4,128]{2,1,0:T(4,128)}, f32[45,4,128]{2,1,0:T(4,128)}, f32[45,4,128]{2,1,0:T(4,128)}) custom-call(f32[32,5,4,128]{3,2,1,0:T(4,128)S(1)} %all_to_all.11.w_ref, f32[45,4,128]{2,1,0:T(4,128)S(1)} %copy-done.2, f32[45,4,128]{2,1,0:T(4,128)S(1)} %copy-done.3, f32[45,4,128]{2,1,0:T(4,128)S(1)} %copy-done.4), custom_call_target="tpu_custom_call" | custom-call | tf_op jit(solution)/shard_map/unpack/pallas_call | solution.py:530
Async XLA Ops:
  0.6 18.8 %copy-start.6 = (f32[9,1,128]{2,1,0:T(1,128)S(1)}, f32[9,1,128]{2,1,0:T(1,128)}, u32[]{:S(2)}) copy-start(f32[9,1,128]{2,1,0:T(1,128)} %constant.15.clone.slope_ref) | copy-start | bytes 13828
  0.6 18.8 %copy-start.7 = (f32[17,2,128]{2,1,0:T(2,128)S(1)}, f32[17,2,128]{2,1,0:T(2,128)}, u32[]{:S(2)}) copy-start(f32[17,2,128]{2,1,0:T(2,128)} %constant.13.clone.tw_ref) | copy-start | bytes 52228
  2.2 17.2 %copy-start = (bf16[768,256]{1,0:T(8,128)(2,1)S(1)}, bf16[768,256]{1,0:T(8,128)(2,1)}, u32[]{:S(2)}) copy-start(bf16[768,256]{1,0:T(8,128)(2,1)} %constant.12.clone.dft_ref) | copy-start | bytes 1179652
  2.2 17.2 %copy-start.1 = (f32[8,4,16,128]{3,2,1,0:T(8,128)S(1)}, f32[8,4,16,128]{3,2,1,0:T(8,128)}, u32[]{:S(2)}) copy-start(f32[8,4,16,128]{3,2,1,0:T(8,128)} %constant.17.clone.band_ref) | copy-start | bytes 786436
  2.2 17.2 %copy-start.5 = (s32[9,1,128]{2,1,0:T(1,128)S(1)}, s32[9,1,128]{2,1,0:T(1,128)}, u32[]{:S(2)}) copy-start(s32[9,1,128]{2,1,0:T(1,128)} %constant.16.clone.least_ref) | copy-start | bytes 13828
  19.4 10.4 %copy-start.8 = (f32[17,2,128]{2,1,0:T(2,128)S(1)}, f32[17,2,128]{2,1,0:T(2,128)}, u32[]{:S(2)}) copy-start(f32[17,2,128]{2,1,0:T(2,128)} %constant.14.clone.tw_ref) | copy-start | bytes 52228
  20.3 7.5 %collective-permute-start = (f32[41,8,128]{2,1,0:T(8,128)S(1)}, f32[41,8,128]{2,1,0:T(8,128)S(1)}, u32[]{:S(2)}, u32[]{:S(2)}) collective-permute-start(f32[41,8,128]{2,1,0:T(8,128)S(1)} %get-tuple-element.13), channel_id=1, source_target_pairs={{0,32},{32,64},{64,96},{96,128},{128,160},{160,192},{192,224},{33,... | collective-permute-start | bytes 503816 | tf_op jit(solution)/shard_map/ppermute | solution.py:514
  22.2 7.6 %collective-permute-start.1 = (f32[41,8,128]{2,1,0:T(8,128)S(1)}, f32[41,8,128]{2,1,0:T(8,128)S(1)}, u32[]{:S(2)}, u32[]{:S(2)}) collective-permute-start(f32[41,8,128]{2,1,0:T(8,128)S(1)} %get-tuple-element.14), channel_id=1, source_target_pairs={{32,0},{64,32},{96,64},{128,96},{160,128},{192,160},{224,192},{1,3... | collective-permute-start | bytes 503816 | tf_op jit(solution)/shard_map/ppermute | solution.py:515
  30.9 17.2 %copy-start.2 = (f32[45,4,128]{2,1,0:T(4,128)S(1)}, f32[45,4,128]{2,1,0:T(4,128)}, u32[]{:S(2)}) copy-start(f32[45,4,128]{2,1,0:T(4,128)} %u_ref.1) | copy-start | bytes 276484
  30.9 17.2 %copy-start.3 = (f32[45,4,128]{2,1,0:T(4,128)S(1)}, f32[45,4,128]{2,1,0:T(4,128)}, u32[]{:S(2)}) copy-start(f32[45,4,128]{2,1,0:T(4,128)} %v_ref.1) | copy-start | bytes 276484
  30.9 17.2 %copy-start.4 = (f32[45,4,128]{2,1,0:T(4,128)S(1)}, f32[45,4,128]{2,1,0:T(4,128)}, u32[]{:S(2)}) copy-start(f32[45,4,128]{2,1,0:T(4,128)} %h_ref.1) | copy-start | bytes 276484
